TPU v7x, 256 devices: a whole 4x4x8 slice. The times are simulated.
256 devices in a mesh: pipe: 16 (over z_lo, x, core), ctx: 16 (over y, z_hi).
Axes of the slice: x: 4, y: 4, z: 8 (z_hi: 4, z_lo: 2; z = z_hi * 2 + z_lo), core: 2. Of those that a mesh axis runs over, the one named last changes fastest.
Arguments:
- queries: bfloat16 [2, 16, 2048, 2560], P(None, 'pipe', 'ctx'), may hold values from -80 to 80
- keys: bfloat16 [2, 16, 2048, 512], P(None, 'pipe', 'ctx'), may hold values from -25 to 25
- values: bfloat16 [2, 16, 2048, 512], P(None, 'pipe', 'ctx'), may hold values from -6 to 6
- grad_a: bfloat16 [16, 2048, 2560], P('pipe', 'ctx'), may hold values from -96 to 96
- grad_b: bfloat16 [16, 2048, 2560], P('pipe', 'ctx'), may hold values from -48 to 48
- imports: int32 [2, 16, 16, 16], P(None, 'pipe'), may hold values from 0 to 1, as said below
- block_ids: int32 [2, 16, 16], P(None, 'pipe'), may hold values from 0 to 15, each once within a row
Outputs:
- dq_a: bfloat16 [16, 2048, 2560], P('pipe', 'ctx')
- dq_b: bfloat16 [16, 2048, 2560], P('pipe', 'ctx')
- kv_grads: bfloat16 [2, 16, 2048, 1024], P(None, 'pipe', 'ctx')
Inputs may be any that keep to these rules, and one draw needn't show every extreme that they name: Every file block sees itself and imports at most 7 other blocks; in each micro-batch and section some block imports exactly 7.
All inputs are finite; a program needn't handle non-finite values.
Results may differ from a plain program's by a relative error of at most 0.015.
Values may be sent and summed in bfloat16 or wider, within the bound.
A program may use at most 64 MiB of HBM per device.

v0:
```python
import math

import jax
import jax.numpy as jnp
from jax import lax
from jax.sharding import PartitionSpec as P

QUERY_HEADS = 20
KEY_VALUE_HEADS = 4
HEAD_DIMENSION = 128
FILE_BLOCK_SIZE = 128
MICRO_BATCHES = 2


negative_large = -1e30


def passed_along(block, axis, distance):
    devices = range(lax.axis_size(axis))
    route = [(i - distance, i) for i in devices if i - distance in devices]
    return lax.ppermute(block, axis, route)


def slot_table(import_mask, block_order):
    blocks_all = block_order.shape[0]
    onehot = (block_order[:, None] == jnp.arange(blocks_all, dtype=jnp.int32)[None, :]).astype(
        jnp.float32
    )
    mapped = jnp.dot(onehot, import_mask.astype(jnp.float32), precision=lax.Precision.HIGHEST)
    return jnp.dot(mapped, onehot.T, precision=lax.Precision.HIGHEST)


def frame_setup(slot_mask, query_start, row_total):
    row_index = query_start + jnp.arange(row_total, dtype=jnp.int32)
    query_slots = row_index // FILE_BLOCK_SIZE
    onehot = (
        query_slots[:, None] == jnp.arange(slot_mask.shape[0], dtype=jnp.int32)[None, :]
    ).astype(jnp.float32)
    reachable = jnp.dot(onehot, slot_mask, precision=lax.Precision.HIGHEST)
    return (reachable, query_slots, row_index % FILE_BLOCK_SIZE)


def tile_mask(frame_info, key_start, key_total_count):
    reachable, query_slots, query_place = frame_info
    key_index = key_start + jnp.arange(key_total_count, dtype=jnp.int32)
    key_slots = key_index // FILE_BLOCK_SIZE
    onehot_keys = (
        key_slots[:, None] == jnp.arange(reachable.shape[1], dtype=jnp.int32)[None, :]
    ).astype(jnp.float32)
    allowed_slot = jnp.dot(reachable, onehot_keys.T, precision=lax.Precision.HIGHEST) > 0.5
    same_slot = query_slots[:, None] == key_slots[None, :]
    causal = (key_index % FILE_BLOCK_SIZE)[None, :] <= query_place[:, None]
    return allowed_slot & (jnp.logical_not(same_slot) | causal)


def over_piece(step_fn, carried, pieces):
    key_fragment, value_fragment = pieces
    piece_rows = key_fragment.shape[0]

    def loop_turn(turn_index, carry_state):
        key_block = lax.dynamic_slice_in_dim(
            key_fragment, turn_index * FILE_BLOCK_SIZE, FILE_BLOCK_SIZE, 0
        )
        value_block = lax.dynamic_slice_in_dim(
            value_fragment, turn_index * FILE_BLOCK_SIZE, FILE_BLOCK_SIZE, 0
        )
        return step_fn(carry_state, key_block, value_block, turn_index * FILE_BLOCK_SIZE)

    return lax.fori_loop(0, piece_rows // FILE_BLOCK_SIZE, loop_turn, carried)


def micro_pass(query_row_tensor, key_rows, value_rows, incoming_gradient, slot_mask, query_start):
    row_total = query_row_tensor.shape[0]
    query_group_width = QUERY_HEADS // KEY_VALUE_HEADS
    softmax_scale = 1.0 / math.sqrt(HEAD_DIMENSION)
    query_head_tensor = query_row_tensor.reshape(
        row_total, KEY_VALUE_HEADS, query_group_width, HEAD_DIMENSION
    )
    gradient_heads = incoming_gradient.reshape(
        row_total, KEY_VALUE_HEADS, query_group_width, HEAD_DIMENSION
    )
    frame_info = frame_setup(slot_mask, query_start, row_total)
    overall_rows = slot_mask.shape[0] * FILE_BLOCK_SIZE

    def stat_step(carried, key_fragment, value_fragment, key_start):
        key_total_count = key_fragment.shape[0]
        allowed = tile_mask(frame_info, key_start, key_total_count)

        def stat_compute_tile(carry_state):
            running_max, running_sum, weighted = carry_state
            key_head_tensor = key_fragment.reshape(key_total_count, KEY_VALUE_HEADS, HEAD_DIMENSION)
            value_head_tensor = value_fragment.reshape(
                key_total_count, KEY_VALUE_HEADS, HEAD_DIMENSION
            )
            scores = (
                jnp.einsum(
                    "rhgd,khd->hgrk",
                    query_head_tensor,
                    key_head_tensor,
                    preferred_element_type=jnp.float32,
                )
                * softmax_scale
            )
            masked = jnp.where(allowed, scores, negative_large)
            new_max = jnp.maximum(running_max, jnp.max(masked, axis=-1))
            weights = jnp.where(allowed, jnp.exp(masked - new_max[..., None]), 0.0)
            rescale = jnp.exp(running_max - new_max)
            running_sum = running_sum * rescale + jnp.sum(weights, axis=-1)
            added = jnp.einsum(
                "hgrk,khd->rhgd",
                weights.astype(jnp.bfloat16),
                value_head_tensor,
                preferred_element_type=jnp.float32,
            )
            weighted = weighted * jnp.transpose(rescale, (2, 0, 1))[..., None] + added
            return (new_max, running_sum, weighted)

        return lax.cond(
            jnp.any(allowed), stat_compute_tile, lambda carry_state: carry_state, carried
        )

    stat_start = (
        jnp.full((KEY_VALUE_HEADS, query_group_width, row_total), negative_large, jnp.float32),
        jnp.zeros((KEY_VALUE_HEADS, query_group_width, row_total), jnp.float32),
        jnp.zeros((row_total, KEY_VALUE_HEADS, query_group_width, HEAD_DIMENSION), jnp.float32),
    )
    stats = over_piece(
        stat_step,
        stat_start,
        (
            lax.all_gather(key_rows, "ctx", axis=0, tiled=True),
            lax.all_gather(value_rows, "ctx", axis=0, tiled=True),
        ),
    )
    running_max, running_sum, weighted = stats
    attended = weighted / jnp.transpose(running_sum, (2, 0, 1))[..., None]
    log_total = running_max + jnp.log(running_sum)
    delta = jnp.transpose(
        jnp.sum(gradient_heads.astype(jnp.float32) * attended, axis=-1), (1, 2, 0)
    )

    def grad_step(carried, key_fragment, value_fragment, key_start):
        key_total_count = key_fragment.shape[0]
        allowed = tile_mask(frame_info, key_start, key_total_count)

        def grad_compute_tile(carry_state):
            q_grad, kv_sums = carry_state
            key_head_tensor = key_fragment.reshape(key_total_count, KEY_VALUE_HEADS, HEAD_DIMENSION)
            value_head_tensor = value_fragment.reshape(
                key_total_count, KEY_VALUE_HEADS, HEAD_DIMENSION
            )
            scores = (
                jnp.einsum(
                    "rhgd,khd->hgrk",
                    query_head_tensor,
                    key_head_tensor,
                    preferred_element_type=jnp.float32,
                )
                * softmax_scale
            )
            probs = jnp.where(
                allowed,
                jnp.exp(jnp.where(allowed, scores - log_total[..., None], negative_large)),
                0.0,
            )
            value_gradient = jnp.einsum(
                "hgrk,rhgd->khd",
                probs.astype(jnp.bfloat16),
                gradient_heads,
                preferred_element_type=jnp.float32,
            )
            prob_grad = jnp.einsum(
                "rhgd,khd->hgrk",
                gradient_heads,
                value_head_tensor,
                preferred_element_type=jnp.float32,
            )
            score_grad = (probs * (prob_grad - delta[..., None])).astype(jnp.bfloat16)
            q_grad = q_grad + jnp.einsum(
                "hgrk,khd->rhgd", score_grad, key_head_tensor, preferred_element_type=jnp.float32
            )
            key_gradient = (
                jnp.einsum(
                    "hgrk,rhgd->khd",
                    score_grad,
                    query_head_tensor,
                    preferred_element_type=jnp.float32,
                )
                * softmax_scale
            )
            update_rows = jnp.concatenate(
                [
                    key_gradient.reshape(key_total_count, KEY_VALUE_HEADS * HEAD_DIMENSION),
                    value_gradient.reshape(key_total_count, KEY_VALUE_HEADS * HEAD_DIMENSION),
                ],
                axis=1,
            )
            previous = lax.dynamic_slice_in_dim(kv_sums, key_start, key_total_count, 0)
            kv_sums = lax.dynamic_update_slice_in_dim(kv_sums, previous + update_rows, key_start, 0)
            return (q_grad, kv_sums)

        return lax.cond(
            jnp.any(allowed), grad_compute_tile, lambda carry_state: carry_state, carried
        )

    grad_start = (
        jnp.zeros((row_total, KEY_VALUE_HEADS, query_group_width, HEAD_DIMENSION), jnp.float32),
        jnp.zeros((overall_rows, 2 * KEY_VALUE_HEADS * HEAD_DIMENSION), jnp.float32),
    )
    q_grad, kv_sums = over_piece(
        grad_step,
        grad_start,
        (
            lax.all_gather(key_rows, "ctx", axis=0, tiled=True),
            lax.all_gather(value_rows, "ctx", axis=0, tiled=True),
        ),
    )
    returned = lax.psum_scatter(
        kv_sums.astype(jnp.bfloat16), "ctx", scatter_dimension=0, tiled=True
    )
    q_result = (
        (q_grad * softmax_scale)
        .reshape(row_total, QUERY_HEADS * HEAD_DIMENSION)
        .astype(jnp.bfloat16)
    )
    return (q_result, returned)


def on_device(queries, keys, values, grad_a, grad_b, imports, block_ids):
    row_total = queries.shape[2]
    query_start = lax.axis_index("ctx") * row_total
    outputs = []
    kv_results = []
    incoming_gradient = grad_a[0]
    for micro_index in range(MICRO_BATCHES):
        if micro_index > 0:
            arrived = passed_along(outputs[0], "pipe", -1)
            incoming_gradient = (
                grad_b[0].astype(jnp.float32) + arrived.astype(jnp.float32)
            ).astype(jnp.bfloat16)
        slot_mask = slot_table(imports[micro_index, 0], block_ids[micro_index, 0])
        q_result, kv_result = micro_pass(
            queries[micro_index, 0],
            keys[micro_index, 0],
            values[micro_index, 0],
            incoming_gradient,
            slot_mask,
            query_start,
        )
        outputs.append(q_result)
        kv_results.append(kv_result)
    return (outputs[0][None], outputs[1][None], jnp.stack(kv_results)[:, None])


def solution(mesh):
    return jax.shard_map(
        on_device,
        mesh=mesh,
        in_specs=(
            P(None, "pipe", "ctx", None),
            P(None, "pipe", "ctx", None),
            P(None, "pipe", "ctx", None),
            P("pipe", "ctx", None),
            P("pipe", "ctx", None),
            P(None, "pipe", None, None),
            P(None, "pipe", None),
        ),
        out_specs=(P("pipe", "ctx", None), P("pipe", "ctx", None), P(None, "pipe", "ctx", None)),
        check_vma=False,
    )
```

profile of v0, /device:TPU:36, one launch (start us, length us, event | category | flops | bytes accessed | tf_op | source)
XLA Modules:
  0.0 522.7 jit_solution(5274312944231669213)
XLA Ops:
  15.3 1.4 fusion.101
  19.5 53.9 %all-gather.9.cloned.1.call-done = bf16[1,1,2048,512]{2,3,1,0:T(8,128)(2,1)} async-done(((bf16[1,1,128,512]{2,3,1,0:T(8,128)(2,1)}), bf16[1,1,2048,512]{2,3,1,0:T(8,128)(2,1)}) %all-gather.9.cloned.1.call-update) | async-done | bytes 2097168 | tf_op jit(solution)/shard_map/all_gather | solution.py:214
  73.4 62.1 %all-gather.11.cloned.1.call-done = bf16[1,1,2048,512]{2,3,1,0:T(8,128)(2,1)} async-done(((bf16[1,1,128,512]{2,3,1,0:T(8,128)(2,1)}), bf16[1,1,2048,512]{2,3,1,0:T(8,128)(2,1)}) %all-gather.11.cloned.1.call-update) | async-done | bytes 2097168 | tf_op jit(solution)/shard_map/all_gather | solution.py:215
  135.6 33.1 %while.80 = (s32[]{:T(128)}, f32[4,5,128]{2,1,0:T(8,128)S(1)}, f32[4,5,128]{2,1,0:T(8,128)S(1)}, f32[128,4,5,128]{3,0,2,1:T(8,128)S(1)}, f32[128,16]{0,1:T(8,128...) while((s32[]{:T(128)}, f32[4,5,128]{2,1,0:T(8,128)S(1)}, ...), condition=%wide.region_6.7_spmd.clone.clone, body=%wide.region_0.6_spmd.clone.clone.sunk | while | flops 174651904 | bytes 8237349 | solution.py:69
  137.2 3.7 conditional.16
  138.2 1.5 fusion.95
  160.2 3.7 conditional.16
  161.2 1.5 fusion.95
  168.7 1.5 copy.61
  170.2 1.5 multiply_reduce_fusion.1
  171.9 4.3 broadcast.931.clone
  176.2 35.9 %while.81 = (s32[]{:T(128)}, f32[128,4,5,128]{3,0,2,1:T(8,128)S(1)}, f32[2048,1024]{0,1:T(8,128)}, f32[128,16]{0,1:T(8,128)S(1)}, bf16[2048,512]{0,1:T(8,128)(2,...) while((s32[]{:T(128)}, ...), condition=%wide.region_12.13_spmd.clone.clone, body=%wide.region_8.12_spmd.clone.clone.sunk | while | flops 425974784 | bytes 14221625 | solution.py:69
  177.8 5.2 %conditional.17 = ((f32[128,4,5,128]{3,0,2,1:T(8,128)S(1)}, f32[2048,1024]{0,1:T(8,128)})) conditional(s32[]{:T(128)} %convert_element_type.212, (f32[128,4,5,128]{3,0,2,1:T(8,128)S(1)}, f32[2048,1024]{0,1:T(8,128)}) %tuple.292, (pred[128,128]{0,1:T(8,128)(4,1)S(1)}, s32[]{:T(128)}, bf16[2048,512]{0,1:T(8,128)(2,1)}, ...), branch_computations={%region_10.10_spmd, %region_11.11_spmd} | conditional | flops 422707200 | bytes 14192706 | solution.py:202
  181.0 2.0 fusion.39
  202.1 5.2 conditional.17
  205.3 2.0 fusion.39
  212.1 1.5 copy.62
  213.6 2.4 multiply_convert_fusion.1
  216.0 28.3 %collective-permute-start = (bf16[128,2560]{0,1:T(8,128)(2,1)}, bf16[128,2560]{0,1:T(8,128)(2,1)}, u32[]{:S(2)}, u32[]{:S(2)}) collective-permute-start(bf16[128,2560]{0,1:T(8,128)(2,1)} %bitcast.61), channel_id=1, source_target_pairs={{16,0},{32,16},{48,32},{64,48},{80,64},{96,80},{112,96},{128,112},... | collective-permute-start | bytes 1966088 | tf_op jit(solution)/shard_map/ppermute | solution.py:21
  244.3 15.4 %all-gather.15.cloned.1.call-done = bf16[1,1,2048,512]{2,3,1,0:T(8,128)(2,1)} async-done(((bf16[1,1,128,512]{2,3,1,0:T(8,128)(2,1)}), bf16[1,1,2048,512]{2,3,1,0:T(8,128)(2,1)}) %all-gather.15.cloned.1.call-update) | async-done | bytes 2097168 | tf_op jit(solution)/shard_map/all_gather | solution.py:215
  259.8 28.2 %while.82 = (s32[]{:T(128)}, f32[4,5,128]{2,1,0:T(8,128)S(1)}, f32[4,5,128]{2,1,0:T(8,128)S(1)}, f32[128,4,5,128]{3,0,2,1:T(8,128)S(1)}, f32[128,16]{0,1:T(8,128...) while((s32[]{:T(128)}, f32[4,5,128]{2,1,0:T(8,128)S(1)}, ...), condition=%wide.region_19.20_spmd.clone.clone, body=%wide.region_13.0_spmd.clone.clone.sunk | while | flops 174651904 | bytes 8237349 | solution.py:69
  261.4 2.6 conditional.18
  288.4 7.3 %copy.70 = bf16[2048,1024]{1,0:T(8,128)(2,1)} copy(f32[2048,1024]{0,1:T(8,128)} %get-tuple-element.1589) | data formatting | bytes 12582912 | tf_op jit(solution)/shard_map/while | solution.py:69
  298.4 4.3 broadcast.931
  302.7 30.7 %while.83 = (s32[]{:T(128)}, f32[128,4,5,128]{3,0,2,1:T(8,128)S(1)}, f32[2048,1024]{0,1:T(8,128)}, f32[128,16]{0,1:T(8,128)S(1)}, bf16[2048,512]{0,1:T(8,128)(2,...) while((s32[]{:T(128)}, ...), condition=%wide.region_25.26_spmd.clone.clone, body=%wide.region_21.25_spmd.clone.clone.sunk | while | flops 425974784 | bytes 14221625 | solution.py:69
  304.3 5.2 %conditional.19 = ((f32[128,4,5,128]{3,0,2,1:T(8,128)S(1)}, f32[2048,1024]{0,1:T(8,128)})) conditional(s32[]{:T(128)} %convert_element_type.214, (f32[128,4,5,128]{3,0,2,1:T(8,128)S(1)}, f32[2048,1024]{0,1:T(8,128)}) %tuple.304, (pred[128,128]{0,1:T(8,128)(4,1)S(1)}, s32[]{:T(128)}, bf16[2048,512]{0,1:T(8,128)(2,1)}, ...), branch_computations={%region_23.23_spmd, %region_24.24_spmd} | conditional | flops 422707200 | bytes 14192706 | solution.py:202
  307.6 2.0 fusion.63
  333.4 7.3 %copy.71 = bf16[2048,1024]{1,0:T(8,128)(2,1)} copy(f32[2048,1024]{0,1:T(8,128)} %get-tuple-element.1590) | data formatting | bytes 12582912 | tf_op jit(solution)/shard_map/while | solution.py:69
  340.8 2.2 copy.72
  344.6 71.5 %reduce-scatter.3.cloned.1.call-done = bf16[128,1024]{1,0:T(8,128)(2,1)} async-done(((bf16[2048,1024]{1,0:T(8,128)(2,1)}), bf16[128,1024]{1,0:T(8,128)(2,1)}) %reduce-scatter.3.cloned.1.call-update) | async-done | bytes 262160 | tf_op jit(solution)/shard_map/reduce_scatter | solution.py:218
  416.1 97.9 %reduce-scatter.5.cloned.1.call-done = bf16[128,1024]{1,0:T(8,128)(2,1)} async-done(((bf16[2048,1024]{1,0:T(8,128)(2,1)}), bf16[128,1024]{1,0:T(8,128)(2,1)}) %reduce-scatter.5.cloned.1.call-update) | async-done | bytes 262160 | tf_op jit(solution)/shard_map/reduce_scatter | solution.py:218
  514.0 1.9 maximum_bitcast_fusion
  (349 shorter events, 90.6 us)
Async XLA Ops:
  7.2 5.4 %copy-start.4 = (s32[2,1,16]{2,1,0:T(1,128)S(1)}, s32[2,1,16]{2,1,0:T(1,128)}, u32[]{:S(2)}) copy-start(s32[2,1,16]{2,1,0:T(1,128)} %param.29) | copy-start | bytes 388
  7.2 5.4 %copy-start.5 = (s32[2,1,16,16]{3,2,1,0:T(8,128)S(1)}, s32[2,1,16,16]{3,2,1,0:T(8,128)}, u32[]{:S(2)}) copy-start(s32[2,1,16,16]{3,2,1,0:T(8,128)} %param.28) | copy-start | bytes 6148
  7.2 66.2 %all-gather.9.cloned.1.call-start = ((), (), s32[]{:S(2)}) async-start(), calls=%async_computation.4 | async-start | bytes 2228224 | tf_op jit(solution)/shard_map/all_gather | solution.py:214
  8.2 5.6 %copy-start.2 = (bf16[1,128,2560]{2,1,0:T(8,128)(2,1)S(1)}, bf16[1,128,2560]{2,1,0:T(8,128)(2,1)}, u32[]{:S(2)}) copy-start(bf16[1,128,2560]{2,1,0:T(8,128)(2,1)} %param.26) | copy-start | bytes 1966084
  9.0 126.5 %all-gather.11.cloned.1.call-start = ((), (), s32[]{:S(2)}) async-start(), calls=%async_computation.5 | async-start | bytes 2228224 | tf_op jit(solution)/shard_map/all_gather | solution.py:215
  10.8 3.4 copy-start.3
  10.8 233.4 %all-gather.13.cloned.1.call-start = ((), (), s32[]{:S(2)}) async-start(), calls=%async_computation.6 | async-start | bytes 2228224 | tf_op jit(solution)/shard_map/all_gather | solution.py:214
  11.7 248.0 %all-gather.15.cloned.1.call-start = ((), (), s32[]{:S(2)}) async-start(), calls=%async_computation.7 | async-start | bytes 2228224 | tf_op jit(solution)/shard_map/all_gather | solution.py:215
  12.5 403.6 %reduce-scatter.3.cloned.1.call-start = ((), (), s32[]{:S(2)}) async-start(), calls=%async_computation.2 | async-start | bytes 4456448 | tf_op jit(solution)/shard_map/reduce_scatter | solution.py:218
  213.6 46.2 %copy-start = (bf16[128,4,5,128]{3,0,2,1:T(8,128)(2,1)S(1)}, bf16[128,4,5,128]{3,0,2,1:T(8,128)(2,1)}, u32[]{:S(2)}) copy-start(bf16[128,4,5,128]{3,0,2,1:T(8,128)(2,1)} %copy.66) | copy-start | bytes 1966084
  216.0 80.0 %collective-permute-start = (bf16[128,2560]{0,1:T(8,128)(2,1)}, bf16[128,2560]{0,1:T(8,128)(2,1)}, u32[]{:S(2)}, u32[]{:S(2)}) collective-permute-start(bf16[128,2560]{0,1:T(8,128)(2,1)} %bitcast.61), channel_id=1, source_target_pairs={{16,0},{32,16},{48,32},{64,48},{80,64},{96,80},{112,96},{128,112},... | collective-permute-start | bytes 1966088 | tf_op jit(solution)/shard_map/ppermute | solution.py:21
  295.7 1.1 copy-start.1
  295.7 218.3 %reduce-scatter.5.cloned.1.call-start = ((), (), s32[]{:S(2)}) async-start(), calls=%async_computation.3 | async-start | bytes 4456448 | tf_op jit(solution)/shard_map/reduce_scatter | solution.py:218
Sparse Core Ops, SparseCore 0:
  11.0 62.3 all-gather.8
  75.8 59.6 all-gather.10
  137.9 59.6 all-gather.12
  199.9 59.7 all-gather.14
  295.8 120.2 reduce-scatter.2
  419.6 94.3 reduce-scatter.4
where the time goes:
time: 527 us; the launch traced here: 523 us
  waiting for transfers between devices  301 us (57%)
  matrix products  69.8 us (13%)
  local copies, waits for them, and re-layouts  48.3 us (9%)
  loops' own time  45 us (9%)
  starting transfers between devices  28.7 us (5%)
  other arithmetic  15.7 us (3%)
  between operations  14.4 us (3%)
    reduce_scatter x2, waiting for transfers between devices, micro_pass(): lax.psum_scatter(kv_sums.astype(jnp.bfloat16), 'ctx', scatter_dimension=0...  169 us
    all_gather x2, waiting for transfers between devices, micro_pass(): lax.all_gather(value_rows, 'ctx', axis=0, tiled=True)  77.5 us
    dot_general x64, matrix products, tile_mask(): jnp.dot(reachable, onehot_keys.T, precision=lax.Precision.HIGHEST) > 0.5  55.8 us
    all_gather x2, waiting for transfers between devices, micro_pass(): lax.all_gather(key_rows, 'ctx', axis=0, tiled=True)  53.9 us
    another operation x4, loops' own time, over_piece(): return lax.fori_loop(0, piece_rows // FILE_BLOCK_SIZE, loop_turn, carried)  43.8 us
    ppermute x1, starting transfers between devices, passed_along(): return lax.ppermute(block, axis, route)  28.3 us
    while x6, local copies, waits for them, and re-layouts, over_piece(): return lax.fori_loop(0, piece_rows // FILE_BLOCK_SIZE, loop_turn, carried)  18.4 us
    unnamed x22, local copies, waits for them, and re-layouts  10.7 us
  transfers between devices with their start and end apart: 7, of which 5 were waited for; matrix products, arithmetic and copies ran while one was open for 25% of the time, Pallas kernels for 0%

commit v1 on v0

v1 whole, which is shorter than its diff:
```python
import functools
import math

import jax
import jax.numpy as jnp
from jax import lax
from jax.experimental import pallas as pl
from jax.experimental.pallas import tpu as pltpu
from jax.sharding import PartitionSpec as P

KEY_VALUE_HEADS = 4
HEAD = 128
GROUP = 5
WIDE = GROUP * HEAD
ROWS = 128
NY = 4
NZ = 4
BLOCKS = NY * NZ
SCALE = 1.0 / math.sqrt(HEAD)
EXP2_SCALE = SCALE * math.log2(math.e)
NEG = -1e30
MESH = pl.DeviceIdType.MESH
BF16 = jnp.bfloat16
F32 = jnp.float32


def place():
    ctx = lax.axis_index("ctx")
    return ctx // NZ, ctx % NZ


def at_ctx(y, z):
    return {"ctx": lax.rem(y, NY) * NZ + lax.rem(z, NZ)}


def cols(index, width):
    return pl.ds(pl.multiple_of(index * width, width), width)


def greet(peers, extra_wait=0):
    barrier = pltpu.get_barrier_semaphore()
    for peer in peers:
        pl.semaphore_signal(barrier, inc=1, device_id=peer, device_id_type=MESH)
    pl.semaphore_wait(barrier, len(peers) + extra_wait)


def remote(src, dst, send, recv, peer):
    return pltpu.make_async_remote_copy(
        src_ref=src, dst_ref=dst, send_sem=send, recv_sem=recv, device_id=peer, device_id_type=MESH
    )


def gather_kernel(
    queries, keys, values, grad_a, grad_b,
    q_a, q_b, up_a, up_b, kv_a, kv_b,
    own_wide, own_kv, wide_send, wide_recv, kv_send, kv_recv, z_send, z_recv, local_in, local_out,
):
    y, z = place()
    greet([at_ctx(y + d, z) for d in range(1, NY)] + [at_ctx(y, z + 1), at_ctx(y, z + NZ - 1)])
    kv_out = (kv_a, kv_b)
    wide_src = (queries.at[0, 0], grad_a.at[0], queries.at[1, 0], grad_b.at[0])
    wide_dst = (q_a, up_a, q_b, up_b)

    kv_copies = {}
    kv_in = []
    for m in range(2):
        for part, source in enumerate((keys, values)):
            own = pltpu.make_async_copy(
                source.at[m, 0, :, cols(y, HEAD)], own_kv.at[2 * m + part], local_in.at[2 * m + part]
            )
            own.start()
            kv_in.append(own)
            for d in range(1, NY):
                there = lax.rem(y + d, NY)
                index = (m * 2 + part) * 3 + d - 1
                copy = remote(
                    source.at[m, 0, :, cols(there, HEAD)],
                    kv_out[m].at[z, part, y],
                    kv_send.at[index],
                    kv_recv.at[index],
                    at_ctx(y + d, z),
                )
                copy.start()
                kv_copies[m, part, d] = copy
    wide_in = []
    wide_copies = []
    for w in range(4):
        own = pltpu.make_async_copy(
            wide_src[w].at[:, cols(y, WIDE)], own_wide.at[w], local_in.at[4 + w]
        )
        own.start()
        wide_in.append(own)
        for d in range(1, NY):
            there = lax.rem(y + d, NY)
            index = w * 3 + d - 1
            copy = remote(
                wide_src[w].at[:, cols(there, WIDE)],
                wide_dst[w].at[y],
                wide_send.at[index],
                wide_recv.at[index],
                at_ctx(y + d, z),
            )
            copy.start()
            wide_copies.append(copy)
    outs = []
    for m in range(2):
        for part in range(2):
            kv_in[2 * m + part].wait()
            out = pltpu.make_async_copy(
                own_kv.at[2 * m + part], kv_out[m].at[z, part, y], local_out.at[2 * m + part]
            )
            out.start()
            outs.append(out)
    for w in range(4):
        wide_in[w].wait()
        out = pltpu.make_async_copy(own_wide.at[w], wide_dst[w].at[y], local_out.at[4 + w])
        out.start()
        outs.append(out)

    up, down = at_ctx(y, z + 1), at_ctx(y, z + NZ - 1)
    before, after = lax.rem(z + NZ - 1, NZ), lax.rem(z + 1, NZ)
    first = {}
    for m in range(2):
        for part in range(2):
            outs[2 * m + part].wait()
            for d in range(1, NY):
                kv_copies[m, part, d].wait_recv()
        for to_up, part in ((1, 0), (0, 1), (1, 1), (0, 0)):
            index = (m * 2 + to_up) * 3 + part
            ref = kv_out[m].at[z, part]
            copy = remote(ref, ref, z_send.at[index], z_recv.at[index], up if to_up else down)
            copy.start()
            first[m, to_up, part] = copy
    second = []
    for m in range(2):
        for to_up, part, owner in ((1, 0, before), (0, 1, after)):
            first[m, to_up, part].wait_recv()
            index = (m * 2 + to_up) * 3 + 2
            ref = kv_out[m].at[owner, part]
            copy = remote(ref, ref, z_send.at[index], z_recv.at[index], up if to_up else down)
            copy.start()
            second.append(copy)
    for m in range(2):
        first[m, 1, 1].wait_recv()
        first[m, 0, 0].wait_recv()
    for copy in second:
        copy.wait_recv()
    for copy in wide_copies:
        copy.wait_recv()
    for out in outs[4:]:
        out.wait()
    for copy in list(kv_copies.values()) + wide_copies + list(first.values()) + second:
        copy.wait_send()


def gather(queries, keys, values, grad_a, grad_b):
    wide = jax.ShapeDtypeStruct((NY, ROWS, WIDE), BF16)
    pair = jax.ShapeDtypeStruct((NZ, 2, NY, ROWS, HEAD), BF16)
    dma = pltpu.SemaphoreType.DMA
    return pl.pallas_call(
        gather_kernel,
        out_shape=(wide, wide, wide, wide, pair, pair),
        in_specs=[pl.BlockSpec(memory_space=pl.ANY)] * 5,
        out_specs=(pl.BlockSpec(memory_space=pl.ANY),) * 6,
        scratch_shapes=[
            pltpu.VMEM((4, ROWS, WIDE), BF16),
            pltpu.VMEM((4, ROWS, HEAD), BF16),
            dma((12,)), dma((12,)), dma((12,)), dma((12,)), dma((12,)), dma((12,)),
            dma((8,)), dma((8,)),
        ],
        compiler_params=pltpu.CompilerParams(collective_id=0, has_side_effects=True),
        name="gather",
    )(queries, keys, values, grad_a, grad_b)


def scatter_kernel(passes, *refs):
    if passes:
        dq_u, dkv, dq_out, kv_out, arrived = refs[:5]
        rest = refs[5:]
    else:
        dq_u, dkv, dq_out, kv_out = refs[:4]
        rest = refs[4:]
    relay, landed, total, q_send, q_recv, z_send, z_recv, k_send, k_recv, local, p_send, p_recv = rest
    y, z = place()
    pipe = lax.axis_index("pipe")
    last = lax.axis_size("pipe") - 1
    barrier = pltpu.get_barrier_semaphore()
    peers = [at_ctx(y + d, z) for d in range(1, NY)] + [at_ctx(y, z + 1), at_ctx(y, z + NZ - 1)]
    for peer in peers:
        pl.semaphore_signal(barrier, inc=1, device_id=peer, device_id_type=MESH)
    if passes:
        @pl.when(pipe < last)
        def _():
            pl.semaphore_signal(barrier, inc=1, device_id={"pipe": pipe + 1}, device_id_type=MESH)

        pl.semaphore_wait(barrier, len(peers) + jnp.where(pipe > 0, 1, 0))
        hand = remote(dq_u, arrived, p_send, p_recv, {"pipe": lax.rem(pipe + last, last + 1)})

        @pl.when(pipe > 0)
        def _():
            hand.start()
    else:
        pl.semaphore_wait(barrier, len(peers))

    up, down = at_ctx(y, z + 1), at_ctx(y, z + NZ - 1)
    before, after = lax.rem(z + NZ - 1, NZ), lax.rem(z + 1, NZ)
    across = lax.rem(z + 2, NZ)

    def z_copy(index, src, dst, peer):
        copy = remote(src, dst, z_send.at[index], z_recv.at[index], peer)
        copy.start()
        return copy

    relay_up = z_copy(0, dkv.at[across, 0], relay.at[0], up)
    relay_down = z_copy(1, dkv.at[across, 1], relay.at[1], down)
    straight_up = z_copy(2, dkv.at[after, 1], landed.at[0], up)
    straight_down = z_copy(3, dkv.at[before, 0], landed.at[1], down)

    q_copies = []
    for d in range(1, NY):
        there = lax.rem(y + d, NY)
        copy = remote(
            dq_u.at[there], dq_out.at[:, cols(y, WIDE)], q_send.at[d - 1], q_recv.at[d - 1],
            at_ctx(y + d, z),
        )
        copy.start()
        q_copies.append(copy)
    own_q = pltpu.make_async_copy(dq_u.at[y], dq_out.at[:, cols(y, WIDE)], local.at[0])
    own_q.start()

    relay_up.wait_recv()
    total[0] = (relay[0].astype(F32) + dkv[after, 0].astype(F32)).astype(BF16)
    sum_up = z_copy(4, total.at[0], landed.at[2], up)
    relay_down.wait_recv()
    total[1] = (relay[1].astype(F32) + dkv[before, 1].astype(F32)).astype(BF16)
    sum_down = z_copy(5, total.at[1], landed.at[3], down)

    straight_down.wait_recv()
    sum_up.wait_recv()
    total[2] = (
        dkv[z, 0].astype(F32) + landed[1].astype(F32) + landed[2].astype(F32)
    ).astype(BF16)
    straight_up.wait_recv()
    sum_down.wait_recv()
    total[3] = (
        dkv[z, 1].astype(F32) + landed[0].astype(F32) + landed[3].astype(F32)
    ).astype(BF16)
    k_copies = []
    own_k = []
    for part in range(2):
        columns = cols(KEY_VALUE_HEADS * part + y, HEAD)
        for d in range(1, NY):
            there = lax.rem(y + d, NY)
            index = part * 3 + d - 1
            copy = remote(
                total.at[2 + part, there], kv_out.at[:, columns], k_send.at[index],
                k_recv.at[index], at_ctx(y + d, z),
            )
            copy.start()
            k_copies.append(copy)
        own = pltpu.make_async_copy(
            total.at[2 + part, y], kv_out.at[:, columns], local.at[1 + part]
        )
        own.start()
        own_k.append(own)
    for copy in q_copies + k_copies:
        copy.wait_recv()
    for copy in [own_q] + own_k:
        copy.wait()
    for copy in q_copies + k_copies + [
        relay_up, relay_down, straight_up, straight_down, sum_up, sum_down
    ]:
        copy.wait_send()
    if passes:
        @pl.when(pipe > 0)
        def _():
            hand.wait_send()

        @pl.when(pipe < last)
        def _():
            hand.wait_recv()


def scatter(dq_u, dkv, passes):
    dma = pltpu.SemaphoreType.DMA
    shapes = [
        jax.ShapeDtypeStruct((ROWS, NY * WIDE), BF16),
        jax.ShapeDtypeStruct((ROWS, 2 * KEY_VALUE_HEADS * HEAD), BF16),
    ]
    if passes:
        shapes.append(jax.ShapeDtypeStruct((NY, ROWS, WIDE), BF16))
    return pl.pallas_call(
        functools.partial(scatter_kernel, passes),
        out_shape=tuple(shapes),
        in_specs=[pl.BlockSpec(memory_space=pltpu.VMEM)] * 2,
        out_specs=(pl.BlockSpec(memory_space=pl.ANY),) * len(shapes),
        scratch_shapes=[
            pltpu.VMEM((2, NY, ROWS, HEAD), BF16),
            pltpu.VMEM((4, NY, ROWS, HEAD), BF16),
            pltpu.VMEM((4, NY, ROWS, HEAD), BF16),
            dma((3,)), dma((3,)), dma((6,)), dma((6,)), dma((6,)), dma((6,)), dma((3,)),
            dma, dma,
        ],
        compiler_params=pltpu.CompilerParams(
            collective_id=1 if passes else 2, has_side_effects=True
        ),
        name="scatter_a" if passes else "scatter_b",
    )(dq_u, dkv)


def nt_dot(a, b):
    return lax.dot_general(a, b, (((1,), (1,)), ((), ())), preferred_element_type=F32)


def attend_kernel(micro, *refs):
    imports, ids, q, upstream = refs[:4]
    if micro:
        arrived, refs = refs[4], refs[5:]
    else:
        refs = refs[4:]
    kv, dq, dkv, scores, grads, sums, q_rows, up_rows, slots = refs
    z = lax.rem(lax.axis_index("ctx"), NZ)
    if micro:
        has_arrived = lax.axis_index("pipe") < lax.axis_size("pipe") - 1
    sums[...] = jnp.zeros_like(sums)
    key_place = lax.broadcasted_iota(jnp.int32, (ROWS, WIDE), 0)
    row_place = lax.rem(lax.broadcasted_iota(jnp.int32, (ROWS, WIDE), 1), ROWS)

    def per_block(i, nothing):
        mine = i * NZ + z
        block = ids[micro, 0, mine]
        slots[0] = mine

        def note(j, count):
            slots[count] = j
            seen = imports[micro, 0, block, ids[micro, 0, j]]
            return count + jnp.where((seen == 1) & (j != mine), 1, 0)

        count = lax.fori_loop(0, BLOCKS, note, jnp.int32(1))
        slots[count] = 0
        for g in range(GROUP):
            span = slice(g * HEAD, (g + 1) * HEAD)
            q_rows[span, :] = q[i, :, span]
            if micro:
                came = jnp.where(has_arrived, arrived[i, :, span].astype(F32), 0.0)
                up_rows[span, :] = (upstream[i, :, span].astype(F32) + came).astype(BF16)
            else:
                up_rows[span, :] = upstream[i, :, span]
        chunks = (count + 1) // 2

        def load(part, c):
            a, b = slots[2 * c], slots[2 * c + 1]
            return jnp.concatenate(
                [kv[lax.rem(a, NZ), part, a // NZ], kv[lax.rem(b, NZ), part, b // NZ]], axis=0
            )

        def first(c, row_max):
            s = nt_dot(load(0, c), q_rows[...]) * EXP2_SCALE
            limit = jnp.where(c == 0, row_place, ROWS)
            top = jnp.where(key_place <= limit, s[:ROWS], NEG)
            bottom = s[ROWS:] + jnp.where(2 * c + 1 < count, 0.0, NEG)
            scores[c, :ROWS] = top
            scores[c, ROWS:] = bottom
            grads[c] = nt_dot(load(1, c), up_rows[...])
            return jnp.maximum(
                row_max, jnp.max(jnp.maximum(top, bottom), axis=0, keepdims=True)
            )

        row_max = lax.fori_loop(0, chunks, first, jnp.full((1, WIDE), NEG, F32))

        def second(c, carry):
            row_sum, inner = carry
            p = jnp.exp2(scores[c] - row_max)
            scores[c] = p
            return (
                row_sum + jnp.sum(p, axis=0, keepdims=True),
                inner + jnp.sum(p * grads[c], axis=0, keepdims=True),
            )

        zero = jnp.zeros((1, WIDE), F32)
        row_sum, inner = lax.fori_loop(0, chunks, second, (zero, zero))
        inverse = 1.0 / row_sum
        delta = inner * inverse

        def third(c, dq_t):
            probs = scores[c] * inverse
            score_grad = (probs * (grads[c] - delta)).astype(BF16)
            dv = jnp.dot(probs.astype(BF16), up_rows[...], preferred_element_type=F32)
            dk = jnp.dot(score_grad, q_rows[...], preferred_element_type=F32) * SCALE
            for half in range(2):
                slot = slots[2 * c + half]
                span = slice(half * ROWS, (half + 1) * ROWS)
                sums[lax.rem(slot, NZ), 0, slot // NZ] += dk[span]
                sums[lax.rem(slot, NZ), 1, slot // NZ] += dv[span]
            return dq_t + lax.dot_general(
                load(0, c), score_grad, (((0,), (0,)), ((), ())), preferred_element_type=F32
            )

        dq_t = lax.fori_loop(0, chunks, third, jnp.zeros((HEAD, WIDE), F32)) * SCALE
        for g in range(GROUP):
            span = slice(g * HEAD, (g + 1) * HEAD)
            dq[i, :, span] = dq_t[:, span].T.astype(BF16)
        return nothing

    lax.fori_loop(0, NY, per_block, 0)
    dkv[...] = sums[...].astype(BF16)


def attend(micro, imports, ids, q, upstream, arrived, kv):
    smem = pl.BlockSpec(memory_space=pltpu.SMEM)
    vmem = pl.BlockSpec(memory_space=pltpu.VMEM)
    arrays = [q, upstream] + ([arrived] if micro else []) + [kv]
    return pl.pallas_call(
        functools.partial(attend_kernel, micro),
        out_shape=(
            jax.ShapeDtypeStruct((NY, ROWS, WIDE), BF16),
            jax.ShapeDtypeStruct((NZ, 2, NY, ROWS, HEAD), BF16),
        ),
        in_specs=[smem, smem] + [vmem] * len(arrays),
        out_specs=(vmem, vmem),
        scratch_shapes=[
            pltpu.VMEM((4, 2 * ROWS, WIDE), F32),
            pltpu.VMEM((4, 2 * ROWS, WIDE), F32),
            pltpu.VMEM((NZ, 2, NY, ROWS, HEAD), F32),
            pltpu.VMEM((WIDE, HEAD), BF16),
            pltpu.VMEM((WIDE, HEAD), BF16),
            pltpu.SMEM((BLOCKS + 2,), jnp.int32),
        ],
        name="attend_b" if micro else "attend_a",
    )(imports, ids, *arrays)


def on_device(queries, keys, values, grad_a, grad_b, imports, block_ids):
    q_a, q_b, up_a, up_b, kv_a, kv_b = gather(queries, keys, values, grad_a, grad_b)
    dq_u, dkv = attend(0, imports, block_ids, q_a, up_a, None, kv_a)
    dq_a, kv_out_a, arrived = scatter(dq_u, dkv, True)
    dq_u, dkv = attend(1, imports, block_ids, q_b, up_b, arrived, kv_b)
    dq_b, kv_out_b = scatter(dq_u, dkv, False)
    return (dq_a[None], dq_b[None], jnp.stack([kv_out_a, kv_out_b])[:, None])


def solution(mesh):
    return jax.shard_map(
        on_device,
        mesh=mesh,
        in_specs=(
            P(None, "pipe", "ctx", None),
            P(None, "pipe", "ctx", None),
            P(None, "pipe", "ctx", None),
            P("pipe", "ctx", None),
            P("pipe", "ctx", None),
            P(None, "pipe", None, None),
            P(None, "pipe", None),
        ),
        out_specs=(P("pipe", "ctx", None), P("pipe", "ctx", None), P(None, "pipe", "ctx", None)),
        check_vma=False,
    )
```

time: 527 us -> 133 us (0.25)
  the two profiles are of different devices: /device:TPU:36 before, /device:TPU:32 now
where the time goes in v1:
time: 133 us; the launch traced here: 131 us
  Pallas kernels  127 us (95%)
  other arithmetic  1.86 us (1%)
  local copies, waits for them, and re-layouts  1.68 us (1%)
    pallas_call x2, Pallas kernels, scatter(): pl.pallas_call(functools.partial(scatter_kernel, passes), out_shape=tuple...  56.3 us
    pallas_call x1, Pallas kernels, gather(): pl.pallas_call(gather_kernel, out_shape=(wide, wide, wide, wide, pair, pa...  48.7 us
    pallas_call x2, Pallas kernels, attend(): pl.pallas_call(functools.partial(attend_kernel, micro), out_shape=(jax.Sh...  22.1 us

profile of v1, /device:TPU:32, one launch (start us, length us, event | category | flops | bytes accessed | tf_op | source)
XLA Modules:
  0.0 131.3 jit_solution(14790993564139788274)
XLA Ops:
  0.6 48.7 %gather.1 = (bf16[4,128,640]{2,1,0:T(8,128)(2,1)}, bf16[4,128,640]{2,1,0:T(8,128)(2,1)}, bf16[4,128,640]{2,1,0:T(8,128)(2,1)}, bf16[4,128,640]{2,1,0:T(8,128)(2,...) custom-call(bf16[2,1,128,2560]{3,2,1,0:T(8,128)(2,1)} %queries.1, ...), custom_call_target="tpu_custom_call" | custom-call | tf_op jit(solution)/shard_map/gather/pallas_call | solution.py:160
  49.3 8.2 %attend_a.1 = (bf16[4,128,640]{2,1,0:T(8,128)(2,1)}, bf16[4,2,4,128,128]{4,3,2,1,0:T(8,128)(2,1)}) custom-call(s32[2,1,16,16]{3,2,1,0:T(8,128)} %refs_0_.3, s32[2,1,16]{2,1,0:T(1,128)} %refs_1_.3, bf16[4,128,640]{2,1,0:T(8,128)(2,1)} %get-tuple-element.18.refs_2_, bf16[4,128,640]{2,1,0:T(8,128)(2,1)} %get-tuple-element.19.refs_3_, ...), custom_call_target="tpu_custom_call" | custom-call | tf_op jit(solution)/shard_map/attend_a/pallas_call | solution.py:413
  57.5 39.0 %scatter_a.1 = (bf16[128,2560]{1,0:T(8,128)(2,1)}, bf16[128,1024]{1,0:T(8,128)(2,1)}, bf16[4,128,640]{2,1,0:T(8,128)(2,1)}) custom-call(bf16[4,128,640]{2,1,0:T(8,128)(2,1)} %get-tuple-element.21.refs_0_, bf16[4,2,4,128,128]{4,3,2,1,0:T(8,128)(2,1)} %get-tuple-element.22.refs_1_), custom_call_target="tpu_custom_call" | custom-call | tf_op jit(solution)/shard_map/scatter_a/pallas_call | solution.py:292
  96.5 13.8 %attend_b.1 = (bf16[4,128,640]{2,1,0:T(8,128)(2,1)}, bf16[4,2,4,128,128]{4,3,2,1,0:T(8,128)(2,1)}) custom-call(s32[2,1,16,16]{3,2,1,0:T(8,128)} %refs_0_.3, s32[2,1,16]{2,1,0:T(1,128)} %refs_1_.3, bf16[4,128,640]{2,1,0:T(8,128)(2,1)} %get-tuple-element.24.refs_2_, bf16[4,128,640]{2,1,0:T(8,128)(2,1)} %get-tuple-element.25.refs_3_, ...), custom_call_target="tpu_custom_call" | custom-call | tf_op jit(solution)/shard_map/attend_b/pallas_call | solution.py:413
  110.3 0.0 copy-start.2
  110.3 0.0 copy-start
  110.3 17.4 %scatter_b.1 = (bf16[128,2560]{1,0:T(8,128)(2,1)}, bf16[128,1024]{1,0:T(8,128)(2,1)}) custom-call(bf16[4,128,640]{2,1,0:T(8,128)(2,1)} %get-tuple-element.28.refs_0_, bf16[4,2,4,128,128]{4,3,2,1,0:T(8,128)(2,1)} %get-tuple-element.29.refs_1_), custom_call_target="tpu_custom_call" | custom-call | tf_op jit(solution)/shard_map/scatter_b/pallas_call | solution.py:292
  127.7 0.0 copy-start.1
  127.7 0.0 copy-done.2
  127.7 1.9 %maximum_bitcast_fusion = bf16[2,1,128,1024]{3,2,1,0:T(8,128)(2,1)} fusion(bf16[1,128,1024]{2,1,0:T(8,128)(2,1)} %bitcast.11, bf16[1,128,1024]{2,1,0:T(8,128)(2,1)S(1)} %bitcast.10), kind=kLoop, calls=%fused_computation | loop fusion | flops 262144 | bytes 1048576
  129.6 0.0 copy-done
  129.6 0.8 copy.13
  130.4 0.0 copy-done.1
  130.4 0.8 copy.14
Async XLA Ops:
  110.3 17.4 %copy-start.2 = (bf16[128,1024]{1,0:T(8,128)(2,1)S(1)}, bf16[128,1024]{1,0:T(8,128)(2,1)}, u32[]{:S(2)}) copy-start(bf16[128,1024]{1,0:T(8,128)(2,1)} %get-tuple-element.31) | copy-start | bytes 786436
  110.3 19.3 %copy-start = (bf16[128,2560]{1,0:T(8,128)(2,1)S(1)}, bf16[128,2560]{1,0:T(8,128)(2,1)}, u32[]{:S(2)}) copy-start(bf16[128,2560]{1,0:T(8,128)(2,1)} %get-tuple-element.23) | copy-start | bytes 1966084
  127.7 2.7 %copy-start.1 = (bf16[128,2560]{1,0:T(8,128)(2,1)S(1)}, bf16[128,2560]{1,0:T(8,128)(2,1)}, u32[]{:S(2)}) copy-start(bf16[128,2560]{1,0:T(8,128)(2,1)} %get-tuple-element.30) | copy-start | bytes 1966084

commit v2 on v0

v2 whole, which is shorter than its diff:
```python
import math

import jax
import jax.numpy as jnp
from jax import lax
from jax.experimental import pallas as pl
from jax.experimental.pallas import tpu as pltpu
from jax.sharding import PartitionSpec as P

KEY_VALUE_HEADS = 4
HEAD = 128
GROUP = 5
WIDE = GROUP * HEAD
ROWS = 128
NY = 4
NZ = 4
BLOCKS = NY * NZ
LISTED = 8
CHUNKS = LISTED // 2
FORWARD_AT = 2
RELAY_AT = 1
SCALE = 1.0 / math.sqrt(HEAD)
EXP2_SCALE = SCALE * math.log2(math.e)
NEG = -1e30
MESH = pl.DeviceIdType.MESH
BF16 = jnp.bfloat16
F32 = jnp.float32


def place():
    ctx = lax.axis_index("ctx")
    return ctx // NZ, ctx % NZ


def at_ctx(y, z):
    return {"ctx": lax.rem(y, NY) * NZ + lax.rem(z, NZ)}


def cols(index, width):
    return pl.ds(pl.multiple_of(index * width, width), width)


def remote(src, dst, send, recv, peer):
    return pltpu.make_async_remote_copy(
        src_ref=src, dst_ref=dst, send_sem=send, recv_sem=recv, device_id=peer, device_id_type=MESH
    )


def nt_dot(a, b):
    return lax.dot_general(a, b, (((1,), (1,)), ((), ())), preferred_element_type=F32)


def list_blocks(micro, z, imports, ids, slots, where_part, counts):
    for i in range(NY):
        mine = i * NZ + z
        block = ids[micro, 0, mine]

        def note(j, carry):
            count, found = carry[0], carry[1:]
            seen = imports[micro, 0, block, ids[micro, 0, j]]
            live = (seen == 1) & (j != mine)
            found = tuple(
                jnp.where(live & (count == p + 1), j, slot) for p, slot in enumerate(found)
            )
            position = jnp.where(live, i * LISTED + count, NY * LISTED)
            where_part[(micro * NY + i) * BLOCKS + j] = jnp.where(
                j == mine, i * LISTED, position
            )
            return (count + jnp.where(live, 1, 0),) + found

        start = (jnp.int32(1),) + (jnp.int32(0),) * (LISTED - 1)
        carry = lax.fori_loop(0, BLOCKS, note, start)
        base = (micro * NY + i) * LISTED
        counts[micro * NY + i] = carry[0]
        slots[base] = mine
        for p in range(LISTED - 1):
            slots[base + p + 1] = carry[p + 1]


def attend_block(micro, i, key_place, row_place, slots, counts, kv, q_rows, up_rows, scores,
                 grads, parts, dq_u):
    base = (micro * NY + i) * LISTED
    count = counts[micro * NY + i]

    def load(part, c):
        a, b = slots[base + 2 * c], slots[base + 2 * c + 1]
        return jnp.concatenate(
            [kv[lax.rem(a, NZ), part, a // NZ], kv[lax.rem(b, NZ), part, b // NZ]], axis=0
        )

    row_max = jnp.full((1, WIDE), NEG, F32)
    for c in range(CHUNKS):
        s = nt_dot(load(0, c), q_rows[...]) * EXP2_SCALE
        if c == 0:
            top = jnp.where(key_place <= row_place, s[:ROWS], NEG)
        else:
            top = s[:ROWS] + jnp.where(2 * c < count, 0.0, NEG)
        bottom = s[ROWS:] + jnp.where(2 * c + 1 < count, 0.0, NEG)
        scores[c, :ROWS] = top
        scores[c, ROWS:] = bottom
        grads[c] = nt_dot(load(1, c), up_rows[...])
        row_max = jnp.maximum(row_max, jnp.max(jnp.maximum(top, bottom), axis=0, keepdims=True))
    row_sum = jnp.zeros((1, WIDE), F32)
    inner = jnp.zeros((1, WIDE), F32)
    for c in range(CHUNKS):
        p = jnp.exp2(scores[c] - row_max)
        scores[c] = p
        row_sum = row_sum + jnp.sum(p, axis=0, keepdims=True)
        inner = inner + jnp.sum(p * grads[c], axis=0, keepdims=True)
    inverse = 1.0 / row_sum
    delta = inner * inverse
    dq_t = jnp.zeros((HEAD, WIDE), F32)
    for c in range(CHUNKS):
        probs = scores[c] * inverse
        score_grad = (probs * (grads[c] - delta)).astype(BF16)
        dv = jnp.dot(probs.astype(BF16), up_rows[...], preferred_element_type=F32)
        dk = jnp.dot(score_grad, q_rows[...], preferred_element_type=F32) * SCALE
        for half in range(2):
            span = slice(half * ROWS, (half + 1) * ROWS)
            parts[i * LISTED + 2 * c + half, 0] = dk[span]
            parts[i * LISTED + 2 * c + half, 1] = dv[span]
        dq_t = dq_t + lax.dot_general(
            load(0, c), score_grad, (((0,), (0,)), ((), ())), preferred_element_type=F32
        )
    dq_t = dq_t * SCALE
    for g in range(GROUP):
        span = slice(g * HEAD, (g + 1) * HEAD)
        dq_u[i, :, span] = dq_t[:, span].T.astype(BF16)


def step_kernel(
    queries, keys, values, grad_a, grad_b, imports, ids,
    dq_out_a, dq_out_b, kv_out,
    q_a, q_b, up_a, up_b, kv_a, kv_b, arrived, dq_u_a, dq_u_b, dkv_a, dkv_b,
    relay_a, relay_b, landed_a, landed_b, total_a, total_b,
    scores, grads, parts, q_rows, up_rows,
    slots, where_part, counts,
    wide_send, wide_recv, kv_send, kv_recv, z_send, z_recv, local_in,
    hand_send, hand_recv, dq_send, dq_recv, r_send, r_recv, o_send, o_recv, local_out,
):
    y, z = place()
    pipe = lax.axis_index("pipe")
    last = lax.axis_size("pipe") - 1
    up, down = at_ctx(y, z + 1), at_ctx(y, z + NZ - 1)
    before, after = lax.rem(z + NZ - 1, NZ), lax.rem(z + 1, NZ)
    across = lax.rem(z + 2, NZ)
    barrier = pltpu.get_barrier_semaphore()
    peers = [at_ctx(y + d, z) for d in range(1, NY)] + [up, down]
    for peer in peers:
        pl.semaphore_signal(barrier, inc=1, device_id=peer, device_id_type=MESH)

    @pl.when(pipe < last)
    def _():
        pl.semaphore_signal(barrier, inc=1, device_id={"pipe": pipe + 1}, device_id_type=MESH)

    pl.semaphore_wait(barrier, len(peers) + jnp.where(pipe > 0, 1, 0))

    kvs = (kv_a, kv_b)
    wide_src = (queries.at[0, 0], grad_a.at[0], queries.at[1, 0], grad_b.at[0])
    wide_dst = (q_a, up_a, q_b, up_b)
    kv_copies, kv_own, wide_copies, wide_own = {}, {}, {}, {}
    for m in range(2):
        for part, source in enumerate((keys, values)):
            for d in range(1, NY):
                there = lax.rem(y + d, NY)
                index = (m * 2 + part) * 3 + d - 1
                kv_copies[m, part, d] = remote(
                    source.at[m, 0, :, cols(there, HEAD)], kvs[m].at[z, part, y],
                    kv_send.at[index], kv_recv.at[index], at_ctx(y + d, z),
                )
                kv_copies[m, part, d].start()
            kv_own[m, part] = pltpu.make_async_copy(
                source.at[m, 0, :, cols(y, HEAD)], kvs[m].at[z, part, y],
                local_in.at[2 * m + part],
            )
            kv_own[m, part].start()
        for w in (2 * m, 2 * m + 1):
            for d in range(1, NY):
                there = lax.rem(y + d, NY)
                index = w * 3 + d - 1
                wide_copies[w, d] = remote(
                    wide_src[w].at[:, cols(there, WIDE)], wide_dst[w].at[y],
                    wide_send.at[index], wide_recv.at[index], at_ctx(y + d, z),
                )
                wide_copies[w, d].start()
            wide_own[w] = pltpu.make_async_copy(
                wide_src[w].at[:, cols(y, WIDE)], wide_dst[w].at[y], local_in.at[4 + w]
            )
            wide_own[w].start()

    def spread(m):
        for part in range(2):
            kv_own[m, part].wait()
            for d in range(1, NY):
                kv_copies[m, part, d].wait_recv()
        for to_up, part in ((1, 0), (0, 1), (1, 1), (0, 0)):
            z_copy(m, to_up, part, part, z).start()

    def z_copy(m, to_up, index, part, owner):
        ref = kvs[m].at[owner, part]
        where = (m * 2 + to_up) * 3 + index
        return remote(ref, ref, z_send.at[where], z_recv.at[where], up if to_up else down)

    def forward(m):
        for to_up, part, owner in ((1, 0, before), (0, 1, after)):
            z_copy(m, to_up, part, part, z).wait_recv()
            z_copy(m, to_up, 2, part, owner).start()

    def wait_spread(m):
        z_copy(m, 1, 1, 1, z).wait_recv()
        z_copy(m, 0, 0, 0, z).wait_recv()
        z_copy(m, 1, 2, 0, across).wait_recv()
        z_copy(m, 0, 2, 1, across).wait_recv()
        for w in (2 * m, 2 * m + 1):
            wide_own[w].wait()
            for d in range(1, NY):
                wide_copies[w, d].wait_recv()

    def hand(i):
        return remote(
            dq_u_a.at[i], arrived.at[i], hand_send.at[i], hand_recv.at[i],
            {"pipe": lax.rem(pipe + last, last + 1)},
        )

    def dq_copy(m, sender, target):
        return remote(
            (dq_u_a, dq_u_b)[m].at[target],
            (dq_out_a, dq_out_b)[m].at[0, :, cols(sender, WIDE)],
            dq_send.at[m * NY + target], dq_recv.at[m * NY + sender], at_ctx(target, z),
        )

    def dq_own(m):
        return pltpu.make_async_copy(
            (dq_u_a, dq_u_b)[m].at[y], (dq_out_a, dq_out_b)[m].at[0, :, cols(y, WIDE)],
            local_out.at[m],
        )

    def return_dq(m, i):
        @pl.when(i == y)
        def _():
            dq_own(m).start()

        @pl.when(i != y)
        def _():
            dq_copy(m, y, i).start()

    def combine(m, dkv):
        def one(slot, nothing):
            places = [where_part[(m * NY + i) * BLOCKS + slot] for i in range(NY)]
            for part in range(2):
                value = parts[places[0], part]
                for at in places[1:]:
                    value = value + parts[at, part]
                dkv[lax.rem(slot, NZ), part, slot // NZ] = value.astype(BF16)
            return nothing

        lax.fori_loop(0, BLOCKS, one, 0)

    relays, landeds, totals, dkvs = (
        (relay_a, relay_b), (landed_a, landed_b), (total_a, total_b), (dkv_a, dkv_b),
    )

    def r_copy(m, index):
        relay, landed, total, dkv = relays[m], landeds[m], totals[m], dkvs[m]
        src, dst, peer = (
            (dkv.at[across, 0], relay.at[0], up),
            (dkv.at[across, 1], relay.at[1], down),
            (dkv.at[after, 1], landed.at[0], up),
            (dkv.at[before, 0], landed.at[1], down),
            (total.at[0], landed.at[2], up),
            (total.at[1], landed.at[3], down),
        )[index]
        return remote(src, dst, r_send.at[m * 6 + index], r_recv.at[m * 6 + index], peer)

    def reduce_start(m):
        for index in range(4):
            r_copy(m, index).start()

    def reduce_relay(m):
        relay, total, dkv = relays[m], totals[m], dkvs[m]
        r_copy(m, 0).wait_recv()
        total[0] = (relay[0].astype(F32) + dkv[after, 0].astype(F32)).astype(BF16)
        r_copy(m, 4).start()
        r_copy(m, 1).wait_recv()
        total[1] = (relay[1].astype(F32) + dkv[before, 1].astype(F32)).astype(BF16)
        r_copy(m, 5).start()

    def o_copy(m, part, sender, target):
        return remote(
            totals[m].at[2 + part, target],
            kv_out.at[m, 0, :, cols(KEY_VALUE_HEADS * part + sender, HEAD)],
            o_send.at[(m * 2 + part) * NY + target], o_recv.at[(m * 2 + part) * NY + sender],
            at_ctx(target, z),
        )

    def o_own(m, part):
        return pltpu.make_async_copy(
            totals[m].at[2 + part, y],
            kv_out.at[m, 0, :, cols(KEY_VALUE_HEADS * part + y, HEAD)],
            local_out.at[2 + 2 * m + part],
        )

    def reduce_end(m):
        landed, total, dkv = landeds[m], totals[m], dkvs[m]
        for part, straight, summed in ((0, 3, 4), (1, 2, 5)):
            r_copy(m, straight).wait_recv()
            r_copy(m, summed).wait_recv()
            total[2 + part] = (
                dkv[z, part].astype(F32)
                + landed[1 - part].astype(F32)
                + landed[2 + part].astype(F32)
            ).astype(BF16)
            for d in range(1, NY):
                o_copy(m, part, y, lax.rem(y + d, NY)).start()
            o_own(m, part).start()

    key_place = lax.broadcasted_iota(jnp.int32, (ROWS, WIDE), 0)
    row_place = lax.rem(lax.broadcasted_iota(jnp.int32, (ROWS, WIDE), 1), ROWS)
    parts[NY * LISTED] = jnp.zeros_like(parts[NY * LISTED])
    for m in range(2):
        list_blocks(m, z, imports, ids, slots, where_part, counts)

    spread(0)
    forward(0)
    spread(1)
    wait_spread(0)

    def turn_a(i, nothing):
        for g in range(GROUP):
            span = slice(g * HEAD, (g + 1) * HEAD)
            q_rows[span, :] = q_a[i, :, span]
            up_rows[span, :] = up_a[i, :, span]
        attend_block(0, i, key_place, row_place, slots, counts, kv_a, q_rows, up_rows, scores,
                     grads, parts, dq_u_a)

        @pl.when(pipe > 0)
        def _():
            hand(i).start()

        return_dq(0, i)

        @pl.when(i == FORWARD_AT)
        def _():
            forward(1)

        return nothing

    lax.fori_loop(0, NY, turn_a, 0)
    combine(0, dkv_a)
    reduce_start(0)
    wait_spread(1)

    def turn_b(i, nothing):
        @pl.when(pipe < last)
        def _():
            hand(i).wait_recv()

        for g in range(GROUP):
            span = slice(g * HEAD, (g + 1) * HEAD)
            q_rows[span, :] = q_b[i, :, span]
            came = jnp.where(pipe < last, arrived[i, :, span].astype(F32), 0.0)
            up_rows[span, :] = (up_b[i, :, span].astype(F32) + came).astype(BF16)
        attend_block(1, i, key_place, row_place, slots, counts, kv_b, q_rows, up_rows, scores,
                     grads, parts, dq_u_b)
        return_dq(1, i)

        @pl.when(i == RELAY_AT)
        def _():
            reduce_relay(0)

        return nothing

    lax.fori_loop(0, NY, turn_b, 0)
    combine(1, dkv_b)
    reduce_start(1)
    reduce_end(0)
    reduce_relay(1)
    reduce_end(1)

    for m in range(2):
        dq_own(m).wait()
        for d in range(1, NY):
            other = lax.rem(y + d, NY)
            dq_copy(m, other, y).wait_recv()
            dq_copy(m, y, other).wait_send()
            for part in range(2):
                o_copy(m, part, other, y).wait_recv()
                o_copy(m, part, y, other).wait_send()
        for part in range(2):
            o_own(m, part).wait()
        for index in range(6):
            r_copy(m, index).wait_send()
        for to_up, part, owner in ((1, 0, before), (0, 1, after)):
            z_copy(m, to_up, 0, 0, z).wait_send()
            z_copy(m, to_up, 1, 1, z).wait_send()
            z_copy(m, to_up, 2, part, owner).wait_send()
    for copy in list(kv_copies.values()) + list(wide_copies.values()):
        copy.wait_send()

    @pl.when(pipe > 0)
    def _():
        for i in range(NY):
            hand(i).wait_send()


def on_device(queries, keys, values, grad_a, grad_b, imports, block_ids):
    wide = pltpu.VMEM((NY, ROWS, WIDE), BF16)
    pair = pltpu.VMEM((NZ, 2, NY, ROWS, HEAD), BF16)
    column = lambda n: pltpu.VMEM((n, NY, ROWS, HEAD), BF16)
    dma = lambda n: pltpu.SemaphoreType.DMA((n,))
    chunk = pltpu.VMEM((CHUNKS, 2 * ROWS, WIDE), F32)
    rows = pltpu.VMEM((WIDE, HEAD), BF16)
    whole = pl.BlockSpec(memory_space=pl.ANY)
    smem = pl.BlockSpec(memory_space=pltpu.SMEM)
    return pl.pallas_call(
        step_kernel,
        out_shape=(
            jax.ShapeDtypeStruct(grad_a.shape, BF16),
            jax.ShapeDtypeStruct(grad_b.shape, BF16),
            jax.ShapeDtypeStruct((2, 1, ROWS, 2 * KEY_VALUE_HEADS * HEAD), BF16),
        ),
        in_specs=[whole] * 5 + [smem, smem],
        out_specs=(whole,) * 3,
        scratch_shapes=[
            wide, wide, wide, wide, pair, pair, wide, wide, wide, pair, pair,
            column(2), column(2), column(4), column(4), column(4), column(4),
            chunk, chunk, pltpu.VMEM((NY * LISTED + 1, 2, ROWS, HEAD), F32), rows, rows,
            pltpu.SMEM((2 * NY * LISTED,), jnp.int32),
            pltpu.SMEM((2 * NY * BLOCKS,), jnp.int32),
            pltpu.SMEM((2 * NY,), jnp.int32),
            dma(12), dma(12), dma(12), dma(12), dma(12), dma(12), dma(8),
            dma(4), dma(4), dma(8), dma(8), dma(12), dma(12), dma(16), dma(16), dma(6),
        ],
        compiler_params=pltpu.CompilerParams(
            collective_id=0, has_side_effects=True, vmem_limit_bytes=60 * 1024 * 1024
        ),
        name="step",
    )(queries, keys, values, grad_a, grad_b, imports, block_ids)


def solution(mesh):
    return jax.shard_map(
        on_device,
        mesh=mesh,
        in_specs=(
            P(None, "pipe", "ctx", None),
            P(None, "pipe", "ctx", None),
            P(None, "pipe", "ctx", None),
            P("pipe", "ctx", None),
            P("pipe", "ctx", None),
            P(None, "pipe", None, None),
            P(None, "pipe", None),
        ),
        out_specs=(P("pipe", "ctx", None), P("pipe", "ctx", None), P(None, "pipe", "ctx", None)),
        check_vma=False,
    )
```

time: 527 us -> 109 us (0.21)
  the two profiles are of different devices: /device:TPU:36 before, /device:TPU:32 now
where the time goes in v2:
time: 109 us; the launch traced here: 108 us
  Pallas kernels  104 us (95%)
  local copies, waits for them, and re-layouts  3.7 us (3%)
    pallas_call x1, Pallas kernels, on_device(): pl.pallas_call(step_kernel, out_shape=(jax.ShapeDtypeStruct(grad_a.shape,...  104 us
    unnamed x7, local copies, waits for them, and re-layouts  3.7 us

profile of v2, /device:TPU:32, one launch (start us, length us, event | category | flops | bytes accessed | tf_op | source)
XLA Modules:
  0.0 108.4 jit_solution(10592214039805941855)
XLA Ops:
  0.6 104.1 %step.1 = (bf16[1,128,2560]{2,1,0:T(8,128)(2,1)}, bf16[1,128,2560]{2,1,0:T(8,128)(2,1)}, bf16[2,1,128,1024]{3,2,1,0:T(8,128)(2,1)}) custom-call(bf16[2,1,128,2560]{3,2,1,0:T(8,128)(2,1)} %queries.1, bf16[2,1,128,512]{3,2,1,0:T(8,128)(2,1)} %keys.1, bf16[2,1,128,512]{3,2,1,0:T(8,128)(2,1)} %values.1, bf16[1,128,2560]{2,1,0:T(8,128)(2,1)} %grad_a.1, ...), custom_call_target="tpu_custom_call" | custom-call | tf_op jit(solution)/shard_map/step/pallas_call | solution.py:415
  104.7 0.0 copy-start
  104.7 0.0 copy-start.1
  104.7 2.1 %copy.13 = bf16[1,128,2560]{2,1,0:T(8,128)(2,1)} copy(bf16[1,128,2560]{2,1,0:T(8,128)(2,1)} %get-tuple-element.6) | data formatting | bytes 1310720
  106.8 0.0 copy-done
  106.8 0.8 copy.14
  107.6 0.0 copy-done.1
  107.6 0.8 copy.15
Async XLA Ops:
  104.7 2.1 %copy-start = (bf16[1,128,2560]{2,1,0:T(8,128)(2,1)S(1)}, bf16[1,128,2560]{2,1,0:T(8,128)(2,1)}, u32[]{:S(2)}) copy-start(bf16[1,128,2560]{2,1,0:T(8,128)(2,1)} %get-tuple-element.7) | copy-start | bytes 1966084
  104.7 2.9 %copy-start.1 = (bf16[2,1,128,1024]{3,2,1,0:T(8,128)(2,1)S(1)}, bf16[2,1,128,1024]{3,2,1,0:T(8,128)(2,1)}, u32[]{:S(2)}) copy-start(bf16[2,1,128,1024]{3,2,1,0:T(8,128)(2,1)} %get-tuple-element.8) | copy-start | bytes 1572868

commit v3 on v2

--- a/solution.py
+++ b/solution.py
@@ -12,6 +12,7 @@
 GROUP = 5
 WIDE = GROUP * HEAD
 ROWS = 128
+HALF = ROWS // 2
 NY = 4
 NZ = 4
 BLOCKS = NY * NZ
@@ -131,16 +132,18 @@
 def step_kernel(
     queries, keys, values, grad_a, grad_b, imports, ids,
     dq_out_a, dq_out_b, kv_out,
-    q_a, q_b, up_a, up_b, kv_a, kv_b, arrived, dq_u_a, dq_u_b, dkv_a, dkv_b,
+    q_a, q_b, up_a, up_b, kv_a, kv_b, arrived, passing, dq_u_a, dq_u_b, dkv_a, dkv_b,
     relay_a, relay_b, landed_a, landed_b, total_a, total_b,
     scores, grads, parts, q_rows, up_rows,
     slots, where_part, counts,
     wide_send, wide_recv, kv_send, kv_recv, z_send, z_recv, local_in,
-    hand_send, hand_recv, dq_send, dq_recv, r_send, r_recv, o_send, o_recv, local_out,
+    hand_send, hand_recv, pass_recv, dq_send, dq_recv, r_send, r_recv, o_send, o_recv, local_out,
 ):
     y, z = place()
     pipe = lax.axis_index("pipe")
     last = lax.axis_size("pipe") - 1
+    edge = (last + 1) // 2
+    spread_hand = edge == 2 * NY
     up, down = at_ctx(y, z + 1), at_ctx(y, z + NZ - 1)
     before, after = lax.rem(z + NZ - 1, NZ), lax.rem(z + 1, NZ)
     across = lax.rem(z + 2, NZ)
@@ -153,7 +156,21 @@
     def _():
         pl.semaphore_signal(barrier, inc=1, device_id={"pipe": pipe + 1}, device_id_type=MESH)
 
-    pl.semaphore_wait(barrier, len(peers) + jnp.where(pipe > 0, 1, 0))
+    callers = len(peers) + jnp.where(pipe > 0, 1, 0)
+    if spread_hand:
+        @pl.when(pipe == edge - 1)
+        def _():
+            for r in range(1, edge):
+                pl.semaphore_signal(
+                    barrier, inc=1, device_id={"pipe": edge + r}, device_id_type=MESH
+                )
+
+        @pl.when(pipe > edge)
+        def _():
+            pl.semaphore_signal(barrier, inc=1, device_id={"pipe": edge}, device_id_type=MESH)
+
+        callers = callers + jnp.where(pipe > edge, 1, 0) + jnp.where(pipe == edge, edge - 1, 0)
+    pl.semaphore_wait(barrier, callers)
 
     kvs = (kv_a, kv_b)
     wide_src = (queries.at[0, 0], grad_a.at[0], queries.at[1, 0], grad_b.at[0])
@@ -216,11 +233,72 @@
             for d in range(1, NY):
                 wide_copies[w, d].wait_recv()
 
-    def hand(i):
+    def hand(i, h):
+        span = pl.ds(h * HALF, HALF)
         return remote(
-            dq_u_a.at[i], arrived.at[i], hand_send.at[i], hand_recv.at[i],
-            {"pipe": lax.rem(pipe + last, last + 1)},
-        )
+            dq_u_a.at[i, span], arrived.at[i, span], hand_send.at[2 * i + h],
+            hand_recv.at[2 * i + h], {"pipe": lax.rem(pipe + last, last + 1)},
+        )
+
+    def to_relay(i, h):
+        return remote(
+            dq_u_a.at[i, pl.ds(h * HALF, HALF)], passing, hand_send.at[2 * i + h],
+            pass_recv.at[0], {"pipe": lax.rem(edge + lax.rem(2 + 2 * i + h, edge), last + 1)},
+        )
+
+    piece = lax.rem(pipe + 2 * edge - 2, 2 * NY)
+
+    def from_relay():
+        i, h = piece // 2, lax.rem(piece, 2)
+        return remote(
+            passing, arrived.at[i, pl.ds(pl.multiple_of(h * HALF, HALF), HALF)],
+            hand_send.at[2 * NY], hand_recv.at[piece], {"pipe": edge - 1},
+        )
+
+    def hand_over(i):
+        direct = (pipe > 0) & (pipe != edge) if spread_hand else pipe > 0
+
+        @pl.when(direct)
+        def _():
+            hand(i, 0).start()
+            hand(i, 1).start()
+
+        if spread_hand:
+            @pl.when(pipe == edge)
+            def _():
+                @pl.when(i < NY - 1)
+                def _():
+                    to_relay(i, 0).start()
+
+                @pl.when(i == NY - 1)
+                def _():
+                    hand(i, 0).start()
+
+                to_relay(i, 1).start()
+
+    def pass_on(i):
+        if spread_hand:
+            @pl.when((pipe > edge) & (piece // 2 + 1 == i))
+            def _():
+                to_relay(0, 0).wait_recv()
+                from_relay().start()
+
+    def hand_end():
+        direct = (pipe > 0) & (pipe <= edge) if spread_hand else pipe > 0
+
+        @pl.when(direct)
+        def _():
+            for i in range(NY):
+                hand(i, 0).wait_send()
+                hand(i, 1).wait_send()
+
+        if spread_hand:
+            @pl.when(pipe > edge)
+            def _():
+                for i in range(NY):
+                    hand(i, 0).wait_send()
+                    hand(i, 1).wait_send()
+                from_relay().wait_send()
 
     def dq_copy(m, sender, target):
         return remote(
@@ -333,11 +411,9 @@
         attend_block(0, i, key_place, row_place, slots, counts, kv_a, q_rows, up_rows, scores,
                      grads, parts, dq_u_a)
 
-        @pl.when(pipe > 0)
-        def _():
-            hand(i).start()
-
+        hand_over(i)
         return_dq(0, i)
+        pass_on(i)
 
         @pl.when(i == FORWARD_AT)
         def _():
@@ -347,13 +423,15 @@
 
     lax.fori_loop(0, NY, turn_a, 0)
     combine(0, dkv_a)
+    pass_on(NY)
     reduce_start(0)
     wait_spread(1)
 
     def turn_b(i, nothing):
         @pl.when(pipe < last)
         def _():
-            hand(i).wait_recv()
+            hand(i, 0).wait_recv()
+            hand(i, 1).wait_recv()
 
         for g in range(GROUP):
             span = slice(g * HEAD, (g + 1) * HEAD)
@@ -397,10 +475,39 @@
     for copy in list(kv_copies.values()) + list(wide_copies.values()):
         copy.wait_send()
 
-    @pl.when(pipe > 0)
-    def _():
-        for i in range(NY):
-            hand(i).wait_send()
+    hand_end()
+
+
+def finish_kernel(*refs):
+    sources, targets, held, sem_in, sem_out = refs[:3], refs[3:6], refs[6:9], refs[9], refs[10]
+    incoming = [
+        pltpu.make_async_copy(source, buffer, sem_in.at[k])
+        for k, (source, buffer) in enumerate(zip(sources, held))
+    ]
+    outgoing = [
+        pltpu.make_async_copy(buffer, target, sem_out.at[k])
+        for k, (buffer, target) in enumerate(zip(held, targets))
+    ]
+    for copy in incoming:
+        copy.start()
+    for copy, later in zip(incoming, outgoing):
+        copy.wait()
+        later.start()
+    for copy in outgoing:
+        copy.wait()
+
+
+def finish(*arrays):
+    whole = pl.BlockSpec(memory_space=pl.ANY)
+    return pl.pallas_call(
+        finish_kernel,
+        out_shape=tuple(jax.ShapeDtypeStruct(a.shape, a.dtype) for a in arrays),
+        in_specs=[whole] * 3,
+        out_specs=(whole,) * 3,
+        scratch_shapes=[pltpu.VMEM(a.shape, a.dtype) for a in arrays]
+        + [pltpu.SemaphoreType.DMA((3,)), pltpu.SemaphoreType.DMA((3,))],
+        name="finish",
+    )(*arrays)
 
 
 def on_device(queries, keys, values, grad_a, grad_b, imports, block_ids):
@@ -412,7 +519,7 @@
     rows = pltpu.VMEM((WIDE, HEAD), BF16)
     whole = pl.BlockSpec(memory_space=pl.ANY)
     smem = pl.BlockSpec(memory_space=pltpu.SMEM)
-    return pl.pallas_call(
+    outputs = pl.pallas_call(
         step_kernel,
         out_shape=(
             jax.ShapeDtypeStruct(grad_a.shape, BF16),
@@ -422,20 +529,22 @@
         in_specs=[whole] * 5 + [smem, smem],
         out_specs=(whole,) * 3,
         scratch_shapes=[
-            wide, wide, wide, wide, pair, pair, wide, wide, wide, pair, pair,
+            wide, wide, wide, wide, pair, pair, wide, pltpu.VMEM((HALF, WIDE), BF16),
+            wide, wide, pair, pair,
             column(2), column(2), column(4), column(4), column(4), column(4),
             chunk, chunk, pltpu.VMEM((NY * LISTED + 1, 2, ROWS, HEAD), F32), rows, rows,
             pltpu.SMEM((2 * NY * LISTED,), jnp.int32),
             pltpu.SMEM((2 * NY * BLOCKS,), jnp.int32),
             pltpu.SMEM((2 * NY,), jnp.int32),
             dma(12), dma(12), dma(12), dma(12), dma(12), dma(12), dma(8),
-            dma(4), dma(4), dma(8), dma(8), dma(12), dma(12), dma(16), dma(16), dma(6),
+            dma(9), dma(8), dma(1), dma(8), dma(8), dma(12), dma(12), dma(16), dma(16), dma(6),
         ],
         compiler_params=pltpu.CompilerParams(
             collective_id=0, has_side_effects=True, vmem_limit_bytes=60 * 1024 * 1024
         ),
         name="step",
     )(queries, keys, values, grad_a, grad_b, imports, block_ids)
+    return finish(*outputs)
 
 
 def solution(mesh):

time: 109 us -> 95.6 us (0.88)
  the two profiles are of different devices: /device:TPU:32 before, /device:TPU:36 now
where the time goes in v3:
time: 95.6 us; the launch traced here: 95.4 us
  Pallas kernels  94.8 us (99%)
    pallas_call x1, Pallas kernels, on_device(): pl.pallas_call(step_kernel, out_shape=(jax.ShapeDtypeStruct(grad_a.shape,...  92.4 us
    pallas_call x1, Pallas kernels, finish(): pl.pallas_call(finish_kernel, out_shape=tuple((jax.ShapeDtypeStruct(a.sha...  2.36 us

profile of v3, /device:TPU:36, one launch (start us, length us, event | category | flops | bytes accessed | tf_op | source)
XLA Modules:
  0.0 95.4 jit_solution(13627635259243223395)
XLA Ops:
  0.6 92.4 %step.1 = (bf16[1,128,2560]{2,1,0:T(8,128)(2,1)}, bf16[1,128,2560]{2,1,0:T(8,128)(2,1)}, bf16[2,1,128,1024]{3,2,1,0:T(8,128)(2,1)}) custom-call(bf16[2,1,128,2560]{3,2,1,0:T(8,128)(2,1)} %queries.1, bf16[2,1,128,512]{3,2,1,0:T(8,128)(2,1)} %keys.1, bf16[2,1,128,512]{3,2,1,0:T(8,128)(2,1)} %values.1, bf16[1,128,2560]{2,1,0:T(8,128)(2,1)} %grad_a.1, ...), custom_call_target="tpu_custom_call" | custom-call | tf_op jit(solution)/shard_map/step/pallas_call | solution.py:522
  93.1 2.4 %finish.1 = (bf16[1,128,2560]{2,1,0:T(8,128)(2,1)}, bf16[1,128,2560]{2,1,0:T(8,128)(2,1)}, bf16[2,1,128,1024]{3,2,1,0:T(8,128)(2,1)}) custom-call(bf16[1,128,2560]{2,1,0:T(8,128)(2,1)} %get-tuple-element.6.refs_0_, bf16[1,128,2560]{2,1,0:T(8,128)(2,1)} %get-tuple-element.7.refs_1_, bf16[2,1,128,1024]{3,2,1,0:T(8,128)(2,1)} %get-tuple-element.8.refs_2_), custom_call_target="tpu_custom_call" | custom-call | tf_op jit(solution)/shard_map/finish/pallas_call | solution.py:502

commit v4 on v3

--- a/solution.py
+++ b/solution.py
@@ -133,11 +133,11 @@
     queries, keys, values, grad_a, grad_b, imports, ids,
     dq_out_a, dq_out_b, kv_out,
     q_a, q_b, up_a, up_b, kv_a, kv_b, arrived, passing, dq_u_a, dq_u_b, dkv_a, dkv_b,
-    relay_a, relay_b, landed_a, landed_b, total_a, total_b,
+    relay_a, relay_b, landed_a, landed_b, summed_a, summed_b, total_a, total_b,
     scores, grads, parts, q_rows, up_rows,
     slots, where_part, counts,
     wide_send, wide_recv, kv_send, kv_recv, z_send, z_recv, local_in,
-    hand_send, hand_recv, pass_recv, dq_send, dq_recv, r_send, r_recv, o_send, o_recv, local_out,
+    hand_send, hand_recv, pass_recv, dq_send, dq_recv, r_send, r_recv, s_send, s_recv, o_send, o_recv, local_out,
 ):
     y, z = place()
     pipe = lax.axis_index("pipe")
@@ -147,6 +147,32 @@
     up, down = at_ctx(y, z + 1), at_ctx(y, z + NZ - 1)
     before, after = lax.rem(z + NZ - 1, NZ), lax.rem(z + 1, NZ)
     across = lax.rem(z + 2, NZ)
+    kvs = (kv_a, kv_b)
+    wide_src = (queries.at[0, 0], grad_a.at[0], queries.at[1, 0], grad_b.at[0])
+    wide_dst = (q_a, up_a, q_b, up_b)
+    kv_copies, kv_own, wide_copies, wide_own = {}, {}, {}, {}
+    for m in range(2):
+        for part, source in enumerate((keys, values)):
+            kv_own[m, part] = pltpu.make_async_copy(
+                source.at[m, 0, :, cols(y, HEAD)], kvs[m].at[z, part, y],
+                local_in.at[2 * m + part],
+            )
+            kv_own[m, part].start()
+    for w in range(4):
+        wide_own[w] = pltpu.make_async_copy(
+            wide_src[w].at[:, cols(y, WIDE)], wide_dst[w].at[y], local_in.at[4 + w]
+        )
+        wide_own[w].start()
+
+    def z_copy(m, to_up, index, part, owner, piece):
+        ref = kvs[m].at[owner, part, piece]
+        where = ((m * 2 + to_up) * 3 + index) * NY + piece
+        return remote(ref, ref, z_send.at[where], z_recv.at[where], up if to_up else down)
+
+    def spread_piece(m, piece):
+        for to_up, part in ((1, 0), (0, 1), (1, 1), (0, 0)):
+            z_copy(m, to_up, part, part, z, piece).start()
+
     barrier = pltpu.get_barrier_semaphore()
     peers = [at_ctx(y + d, z) for d in range(1, NY)] + [up, down]
     for peer in peers:
@@ -172,10 +198,6 @@
         callers = callers + jnp.where(pipe > edge, 1, 0) + jnp.where(pipe == edge, edge - 1, 0)
     pl.semaphore_wait(barrier, callers)
 
-    kvs = (kv_a, kv_b)
-    wide_src = (queries.at[0, 0], grad_a.at[0], queries.at[1, 0], grad_b.at[0])
-    wide_dst = (q_a, up_a, q_b, up_b)
-    kv_copies, kv_own, wide_copies, wide_own = {}, {}, {}, {}
     for m in range(2):
         for part, source in enumerate((keys, values)):
             for d in range(1, NY):
@@ -186,11 +208,6 @@
                     kv_send.at[index], kv_recv.at[index], at_ctx(y + d, z),
                 )
                 kv_copies[m, part, d].start()
-            kv_own[m, part] = pltpu.make_async_copy(
-                source.at[m, 0, :, cols(y, HEAD)], kvs[m].at[z, part, y],
-                local_in.at[2 * m + part],
-            )
-            kv_own[m, part].start()
         for w in (2 * m, 2 * m + 1):
             for d in range(1, NY):
                 there = lax.rem(y + d, NY)
@@ -200,34 +217,30 @@
                     wide_send.at[index], wide_recv.at[index], at_ctx(y + d, z),
                 )
                 wide_copies[w, d].start()
-            wide_own[w] = pltpu.make_async_copy(
-                wide_src[w].at[:, cols(y, WIDE)], wide_dst[w].at[y], local_in.at[4 + w]
-            )
-            wide_own[w].start()
+        if m == 0:
+            for part in range(2):
+                kv_own[0, part].wait()
+            spread_piece(0, y)
 
     def spread(m):
-        for part in range(2):
-            kv_own[m, part].wait()
-            for d in range(1, NY):
-                kv_copies[m, part, d].wait_recv()
-        for to_up, part in ((1, 0), (0, 1), (1, 1), (0, 0)):
-            z_copy(m, to_up, part, part, z).start()
-
-    def z_copy(m, to_up, index, part, owner):
-        ref = kvs[m].at[owner, part]
-        where = (m * 2 + to_up) * 3 + index
-        return remote(ref, ref, z_send.at[where], z_recv.at[where], up if to_up else down)
+        for d in (1, 3, 2):
+            for part in range(2):
+                kv_copies[m, part, NY - d].wait_recv()
+            spread_piece(m, lax.rem(y + d, NY))
 
     def forward(m):
-        for to_up, part, owner in ((1, 0, before), (0, 1, after)):
-            z_copy(m, to_up, part, part, z).wait_recv()
-            z_copy(m, to_up, 2, part, owner).start()
+        for d in (0, 1, 3, 2):
+            piece = lax.rem(y + d, NY)
+            for to_up, part, owner in ((1, 0, before), (0, 1, after)):
+                z_copy(m, to_up, part, part, z, piece).wait_recv()
+                z_copy(m, to_up, 2, part, owner, piece).start()
 
     def wait_spread(m):
-        z_copy(m, 1, 1, 1, z).wait_recv()
-        z_copy(m, 0, 0, 0, z).wait_recv()
-        z_copy(m, 1, 2, 0, across).wait_recv()
-        z_copy(m, 0, 2, 1, across).wait_recv()
+        for b in range(NY):
+            z_copy(m, 1, 1, 1, z, b).wait_recv()
+            z_copy(m, 0, 0, 0, z, b).wait_recv()
+            z_copy(m, 1, 2, 0, across, b).wait_recv()
+            z_copy(m, 0, 2, 1, across, b).wait_recv()
         for w in (2 * m, 2 * m + 1):
             wide_own[w].wait()
             for d in range(1, NY):
@@ -339,16 +352,21 @@
     )
 
     def r_copy(m, index):
-        relay, landed, total, dkv = relays[m], landeds[m], totals[m], dkvs[m]
+        relay, landed, dkv = relays[m], landeds[m], dkvs[m]
         src, dst, peer = (
             (dkv.at[across, 0], relay.at[0], up),
             (dkv.at[across, 1], relay.at[1], down),
             (dkv.at[after, 1], landed.at[0], up),
             (dkv.at[before, 0], landed.at[1], down),
-            (total.at[0], landed.at[2], up),
-            (total.at[1], landed.at[3], down),
         )[index]
-        return remote(src, dst, r_send.at[m * 6 + index], r_recv.at[m * 6 + index], peer)
+        return remote(src, dst, r_send.at[m * 4 + index], r_recv.at[m * 4 + index], peer)
+
+    def s_copy(m, part, turn):
+        where = (m * 2 + part) * NY + turn
+        return remote(
+            totals[m].at[part, turn], (summed_a, summed_b)[m].at[part, turn],
+            s_send.at[where], s_recv.at[where], (up, down)[part],
+        )
 
     def reduce_start(m):
         for index in range(4):
@@ -357,15 +375,18 @@
     def reduce_relay(m):
         relay, total, dkv = relays[m], totals[m], dkvs[m]
         r_copy(m, 0).wait_recv()
-        total[0] = (relay[0].astype(F32) + dkv[after, 0].astype(F32)).astype(BF16)
-        r_copy(m, 4).start()
         r_copy(m, 1).wait_recv()
-        total[1] = (relay[1].astype(F32) + dkv[before, 1].astype(F32)).astype(BF16)
-        r_copy(m, 5).start()
-
-    def o_copy(m, part, sender, target):
+        for turn, d in enumerate((2, 1, 3, 0)):
+            piece = lax.rem(y + d, NY)
+            for part, owner in ((0, after), (1, before)):
+                total[part, turn] = (
+                    relay[part, piece].astype(F32) + dkv[owner, part, piece].astype(F32)
+                ).astype(BF16)
+                s_copy(m, part, turn).start()
+
+    def o_copy(m, part, sender, target, turn=0):
         return remote(
-            totals[m].at[2 + part, target],
+            totals[m].at[2 + part, turn],
             kv_out.at[m, 0, :, cols(KEY_VALUE_HEADS * part + sender, HEAD)],
             o_send.at[(m * 2 + part) * NY + target], o_recv.at[(m * 2 + part) * NY + sender],
             at_ctx(target, z),
@@ -373,34 +394,40 @@
 
     def o_own(m, part):
         return pltpu.make_async_copy(
-            totals[m].at[2 + part, y],
+            totals[m].at[2 + part, NY - 1],
             kv_out.at[m, 0, :, cols(KEY_VALUE_HEADS * part + y, HEAD)],
             local_out.at[2 + 2 * m + part],
         )
 
     def reduce_end(m):
-        landed, total, dkv = landeds[m], totals[m], dkvs[m]
-        for part, straight, summed in ((0, 3, 4), (1, 2, 5)):
-            r_copy(m, straight).wait_recv()
-            r_copy(m, summed).wait_recv()
-            total[2 + part] = (
-                dkv[z, part].astype(F32)
-                + landed[1 - part].astype(F32)
-                + landed[2 + part].astype(F32)
-            ).astype(BF16)
-            for d in range(1, NY):
-                o_copy(m, part, y, lax.rem(y + d, NY)).start()
-            o_own(m, part).start()
+        landed, total, dkv, summed = landeds[m], totals[m], dkvs[m], (summed_a, summed_b)[m]
+        r_copy(m, 2).wait_recv()
+        r_copy(m, 3).wait_recv()
+        for turn, d in enumerate((2, 1, 3, 0)):
+            piece = lax.rem(y + d, NY)
+            for part in range(2):
+                s_copy(m, part, turn).wait_recv()
+                total[2 + part, turn] = (
+                    dkv[z, part, piece].astype(F32)
+                    + landed[1 - part, piece].astype(F32)
+                    + summed[part, turn].astype(F32)
+                ).astype(BF16)
+                if d:
+                    o_copy(m, part, y, piece, turn).start()
+                else:
+                    o_own(m, part).start()
 
     key_place = lax.broadcasted_iota(jnp.int32, (ROWS, WIDE), 0)
     row_place = lax.rem(lax.broadcasted_iota(jnp.int32, (ROWS, WIDE), 1), ROWS)
     parts[NY * LISTED] = jnp.zeros_like(parts[NY * LISTED])
-    for m in range(2):
-        list_blocks(m, z, imports, ids, slots, where_part, counts)
-
     spread(0)
+    list_blocks(0, z, imports, ids, slots, where_part, counts)
     forward(0)
+    for part in range(2):
+        kv_own[1, part].wait()
+    spread_piece(1, y)
     spread(1)
+    list_blocks(1, z, imports, ids, slots, where_part, counts)
     wait_spread(0)
 
     def turn_a(i, nothing):
@@ -466,12 +493,15 @@
                 o_copy(m, part, y, other).wait_send()
         for part in range(2):
             o_own(m, part).wait()
-        for index in range(6):
+        for index in range(4):
             r_copy(m, index).wait_send()
-        for to_up, part, owner in ((1, 0, before), (0, 1, after)):
-            z_copy(m, to_up, 0, 0, z).wait_send()
-            z_copy(m, to_up, 1, 1, z).wait_send()
-            z_copy(m, to_up, 2, part, owner).wait_send()
+        for b in range(NY):
+            for part in range(2):
+                s_copy(m, part, b).wait_send()
+            for to_up, part, owner in ((1, 0, before), (0, 1, after)):
+                z_copy(m, to_up, 0, 0, z, b).wait_send()
+                z_copy(m, to_up, 1, 1, z, b).wait_send()
+                z_copy(m, to_up, 2, part, owner, b).wait_send()
     for copy in list(kv_copies.values()) + list(wide_copies.values()):
         copy.wait_send()
 
@@ -531,13 +561,13 @@
         scratch_shapes=[
             wide, wide, wide, wide, pair, pair, wide, pltpu.VMEM((HALF, WIDE), BF16),
             wide, wide, pair, pair,
-            column(2), column(2), column(4), column(4), column(4), column(4),
+            column(2), column(2), column(2), column(2), column(2), column(2), column(4), column(4),
             chunk, chunk, pltpu.VMEM((NY * LISTED + 1, 2, ROWS, HEAD), F32), rows, rows,
             pltpu.SMEM((2 * NY * LISTED,), jnp.int32),
             pltpu.SMEM((2 * NY * BLOCKS,), jnp.int32),
             pltpu.SMEM((2 * NY,), jnp.int32),
-            dma(12), dma(12), dma(12), dma(12), dma(12), dma(12), dma(8),
-            dma(9), dma(8), dma(1), dma(8), dma(8), dma(12), dma(12), dma(16), dma(16), dma(6),
+            dma(12), dma(12), dma(12), dma(12), dma(48), dma(48), dma(8),
+            dma(9), dma(8), dma(1), dma(8), dma(8), dma(8), dma(8), dma(16), dma(16), dma(16), dma(16), dma(6),
         ],
         compiler_params=pltpu.CompilerParams(
             collective_id=0, has_side_effects=True, vmem_limit_bytes=60 * 1024 * 1024

time: 95.6 us -> 95.1 us (level)
  no operation moved by 1% of the time
where the time goes in v4:
time: 95.1 us; the launch traced here: 95 us
  Pallas kernels  94.3 us (99%)
    pallas_call x1, Pallas kernels, on_device(): pl.pallas_call(step_kernel, out_shape=(jax.ShapeDtypeStruct(grad_a.shape,...  91.9 us
    pallas_call x1, Pallas kernels, finish(): pl.pallas_call(finish_kernel, out_shape=tuple((jax.ShapeDtypeStruct(a.sha...  2.36 us

profile of v4, /device:TPU:36, one launch (start us, length us, event | category | flops | bytes accessed | tf_op | source)
XLA Modules:
  0.0 95.0 jit_solution(9285098505535543579)
XLA Ops:
  0.6 91.9 %step.1 = (bf16[1,128,2560]{2,1,0:T(8,128)(2,1)}, bf16[1,128,2560]{2,1,0:T(8,128)(2,1)}, bf16[2,1,128,1024]{3,2,1,0:T(8,128)(2,1)}) custom-call(bf16[2,1,128,2560]{3,2,1,0:T(8,128)(2,1)} %queries.1, bf16[2,1,128,512]{3,2,1,0:T(8,128)(2,1)} %keys.1, bf16[2,1,128,512]{3,2,1,0:T(8,128)(2,1)} %values.1, bf16[1,128,2560]{2,1,0:T(8,128)(2,1)} %grad_a.1, ...), custom_call_target="tpu_custom_call" | custom-call | tf_op jit(solution)/shard_map/step/pallas_call | solution.py:552
  92.6 2.4 %finish.1 = (bf16[1,128,2560]{2,1,0:T(8,128)(2,1)}, bf16[1,128,2560]{2,1,0:T(8,128)(2,1)}, bf16[2,1,128,1024]{3,2,1,0:T(8,128)(2,1)}) custom-call(bf16[1,128,2560]{2,1,0:T(8,128)(2,1)} %get-tuple-element.6.refs_0_, bf16[1,128,2560]{2,1,0:T(8,128)(2,1)} %get-tuple-element.7.refs_1_, bf16[2,1,128,1024]{3,2,1,0:T(8,128)(2,1)} %get-tuple-element.8.refs_2_), custom_call_target="tpu_custom_call" | custom-call | tf_op jit(solution)/shard_map/finish/pallas_call | solution.py:532

commit v5 on v4

--- a/solution.py
+++ b/solution.py
@@ -19,6 +19,7 @@
 LISTED = 8
 CHUNKS = LISTED // 2
 FORWARD_AT = 2
+PIECES = 4
 RELAY_AT = 1
 SCALE = 1.0 / math.sqrt(HEAD)
 EXP2_SCALE = SCALE * math.log2(math.e)
@@ -198,29 +199,36 @@
         callers = callers + jnp.where(pipe > edge, 1, 0) + jnp.where(pipe == edge, edge - 1, 0)
     pl.semaphore_wait(barrier, callers)
 
-    for m in range(2):
-        for part, source in enumerate((keys, values)):
-            for d in range(1, NY):
-                there = lax.rem(y + d, NY)
+    def start_kv(m):
+        for d in range(1, NY):
+            there = lax.rem(y + d, NY)
+            for part, source in enumerate((keys, values)):
                 index = (m * 2 + part) * 3 + d - 1
                 kv_copies[m, part, d] = remote(
                     source.at[m, 0, :, cols(there, HEAD)], kvs[m].at[z, part, y],
                     kv_send.at[index], kv_recv.at[index], at_ctx(y + d, z),
                 )
                 kv_copies[m, part, d].start()
-        for w in (2 * m, 2 * m + 1):
-            for d in range(1, NY):
-                there = lax.rem(y + d, NY)
-                index = w * 3 + d - 1
-                wide_copies[w, d] = remote(
-                    wide_src[w].at[:, cols(there, WIDE)], wide_dst[w].at[y],
-                    wide_send.at[index], wide_recv.at[index], at_ctx(y + d, z),
-                )
-                wide_copies[w, d].start()
-        if m == 0:
-            for part in range(2):
-                kv_own[0, part].wait()
-            spread_piece(0, y)
+
+    def start_wide(w):
+        for d in range(1, NY):
+            there = lax.rem(y + d, NY)
+            index = w * 3 + d - 1
+            wide_copies[w, d] = remote(
+                wide_src[w].at[:, cols(there, WIDE)], wide_dst[w].at[y],
+                wide_send.at[index], wide_recv.at[index], at_ctx(y + d, z),
+            )
+            wide_copies[w, d].start()
+
+    start_kv(0)
+    for part in range(2):
+        kv_own[0, part].wait()
+    spread_piece(0, y)
+    start_kv(1)
+    start_wide(0)
+    start_wide(1)
+    start_wide(2)
+    start_wide(3)
 
     def spread(m):
         for d in (1, 3, 2):
@@ -228,8 +236,8 @@
                 kv_copies[m, part, NY - d].wait_recv()
             spread_piece(m, lax.rem(y + d, NY))
 
-    def forward(m):
-        for d in (0, 1, 3, 2):
+    def forward(m, order=(0, 1, 3, 2)):
+        for d in order:
             piece = lax.rem(y + d, NY)
             for to_up, part, owner in ((1, 0, before), (0, 1, after)):
                 z_copy(m, to_up, part, part, z, piece).wait_recv()
@@ -442,9 +450,13 @@
         return_dq(0, i)
         pass_on(i)
 
+        @pl.when(i == FORWARD_AT - 1)
+        def _():
+            forward(1, (0, 1))
+
         @pl.when(i == FORWARD_AT)
         def _():
-            forward(1)
+            forward(1, (3, 2))
 
         return nothing
 
@@ -510,14 +522,20 @@
 
 def finish_kernel(*refs):
     sources, targets, held, sem_in, sem_out = refs[:3], refs[3:6], refs[6:9], refs[9], refs[10]
-    incoming = [
-        pltpu.make_async_copy(source, buffer, sem_in.at[k])
-        for k, (source, buffer) in enumerate(zip(sources, held))
-    ]
-    outgoing = [
-        pltpu.make_async_copy(buffer, target, sem_out.at[k])
-        for k, (buffer, target) in enumerate(zip(held, targets))
-    ]
+    incoming, outgoing = [], []
+    for k, (source, target, buffer) in enumerate(zip(sources, targets, held)):
+        rows = ROWS // PIECES
+        for lead in range(source.shape[0]):
+            for p in range(PIECES):
+                middle = (0,) * (len(source.shape) - 3)
+                at = (lead,) + middle + (pl.ds(p * rows, rows),)
+                n = len(incoming)
+                incoming.append(
+                    pltpu.make_async_copy(source.at[at], buffer.at[at], sem_in.at[n])
+                )
+                outgoing.append(
+                    pltpu.make_async_copy(buffer.at[at], target.at[at], sem_out.at[n])
+                )
     for copy in incoming:
         copy.start()
     for copy, later in zip(incoming, outgoing):
@@ -535,7 +553,7 @@
         in_specs=[whole] * 3,
         out_specs=(whole,) * 3,
         scratch_shapes=[pltpu.VMEM(a.shape, a.dtype) for a in arrays]
-        + [pltpu.SemaphoreType.DMA((3,)), pltpu.SemaphoreType.DMA((3,))],
+        + [pltpu.SemaphoreType.DMA((4 * PIECES,)), pltpu.SemaphoreType.DMA((4 * PIECES,))],
         name="finish",
     )(*arrays)
 

time: 95.1 us -> 93.4 us (0.982)
  Pallas kernels: 94.3 us -> 91.8 us
    pallas_call x1, Pallas kernels: 91.9 us -> 89.3 us  [on_device(): pl.pallas_call(step_kernel, out_shape=(jax.ShapeDtypeStruct(grad_a.shape,...]
where the time goes in v5:
time: 93.4 us; the launch traced here: 92.4 us
  Pallas kernels  91.8 us (98%)
    pallas_call x1, Pallas kernels, on_device(): pl.pallas_call(step_kernel, out_shape=(jax.ShapeDtypeStruct(grad_a.shape,...  89.3 us
    pallas_call x1, Pallas kernels, finish(): pl.pallas_call(finish_kernel, out_shape=tuple((jax.ShapeDtypeStruct(a.sha...  2.51 us

profile of v5, /device:TPU:36, one launch (start us, length us, event | category | flops | bytes accessed | tf_op | source)
XLA Modules:
  0.0 92.4 jit_solution(5741065037246058096)
XLA Ops:
  0.6 89.3 %step.1 = (bf16[1,128,2560]{2,1,0:T(8,128)(2,1)}, bf16[1,128,2560]{2,1,0:T(8,128)(2,1)}, bf16[2,1,128,1024]{3,2,1,0:T(8,128)(2,1)}) custom-call(bf16[2,1,128,2560]{3,2,1,0:T(8,128)(2,1)} %queries.1, bf16[2,1,128,512]{3,2,1,0:T(8,128)(2,1)} %keys.1, bf16[2,1,128,512]{3,2,1,0:T(8,128)(2,1)} %values.1, bf16[1,128,2560]{2,1,0:T(8,128)(2,1)} %grad_a.1, ...), custom_call_target="tpu_custom_call" | custom-call | tf_op jit(solution)/shard_map/step/pallas_call | solution.py:570
  89.9 2.5 %finish.1 = (bf16[1,128,2560]{2,1,0:T(8,128)(2,1)}, bf16[1,128,2560]{2,1,0:T(8,128)(2,1)}, bf16[2,1,128,1024]{3,2,1,0:T(8,128)(2,1)}) custom-call(bf16[1,128,2560]{2,1,0:T(8,128)(2,1)} %get-tuple-element.6.refs_0_, bf16[1,128,2560]{2,1,0:T(8,128)(2,1)} %get-tuple-element.7.refs_1_, bf16[2,1,128,1024]{3,2,1,0:T(8,128)(2,1)} %get-tuple-element.8.refs_2_), custom_call_target="tpu_custom_call" | custom-call | tf_op jit(solution)/shard_map/finish/pallas_call | solution.py:550

commit v6 on v5

--- a/solution.py
+++ b/solution.py
@@ -19,7 +19,6 @@
 LISTED = 8
 CHUNKS = LISTED // 2
 FORWARD_AT = 2
-PIECES = 4
 RELAY_AT = 1
 SCALE = 1.0 / math.sqrt(HEAD)
 EXP2_SCALE = SCALE * math.log2(math.e)
@@ -520,44 +519,6 @@
     hand_end()
 
 
-def finish_kernel(*refs):
-    sources, targets, held, sem_in, sem_out = refs[:3], refs[3:6], refs[6:9], refs[9], refs[10]
-    incoming, outgoing = [], []
-    for k, (source, target, buffer) in enumerate(zip(sources, targets, held)):
-        rows = ROWS // PIECES
-        for lead in range(source.shape[0]):
-            for p in range(PIECES):
-                middle = (0,) * (len(source.shape) - 3)
-                at = (lead,) + middle + (pl.ds(p * rows, rows),)
-                n = len(incoming)
-                incoming.append(
-                    pltpu.make_async_copy(source.at[at], buffer.at[at], sem_in.at[n])
-                )
-                outgoing.append(
-                    pltpu.make_async_copy(buffer.at[at], target.at[at], sem_out.at[n])
-                )
-    for copy in incoming:
-        copy.start()
-    for copy, later in zip(incoming, outgoing):
-        copy.wait()
-        later.start()
-    for copy in outgoing:
-        copy.wait()
-
-
-def finish(*arrays):
-    whole = pl.BlockSpec(memory_space=pl.ANY)
-    return pl.pallas_call(
-        finish_kernel,
-        out_shape=tuple(jax.ShapeDtypeStruct(a.shape, a.dtype) for a in arrays),
-        in_specs=[whole] * 3,
-        out_specs=(whole,) * 3,
-        scratch_shapes=[pltpu.VMEM(a.shape, a.dtype) for a in arrays]
-        + [pltpu.SemaphoreType.DMA((4 * PIECES,)), pltpu.SemaphoreType.DMA((4 * PIECES,))],
-        name="finish",
-    )(*arrays)
-
-
 def on_device(queries, keys, values, grad_a, grad_b, imports, block_ids):
     wide = pltpu.VMEM((NY, ROWS, WIDE), BF16)
     pair = pltpu.VMEM((NZ, 2, NY, ROWS, HEAD), BF16)
@@ -567,14 +528,14 @@
     rows = pltpu.VMEM((WIDE, HEAD), BF16)
     whole = pl.BlockSpec(memory_space=pl.ANY)
     smem = pl.BlockSpec(memory_space=pltpu.SMEM)
-    outputs = pl.pallas_call(
+    return pl.pallas_call(
         step_kernel,
         out_shape=(
             jax.ShapeDtypeStruct(grad_a.shape, BF16),
             jax.ShapeDtypeStruct(grad_b.shape, BF16),
             jax.ShapeDtypeStruct((2, 1, ROWS, 2 * KEY_VALUE_HEADS * HEAD), BF16),
         ),
-        in_specs=[whole] * 5 + [smem, smem],
+        in_specs=[pl.BlockSpec(memory_space=pltpu.HBM)] * 5 + [smem, smem],
         out_specs=(whole,) * 3,
         scratch_shapes=[
             wide, wide, wide, wide, pair, pair, wide, pltpu.VMEM((HALF, WIDE), BF16),
@@ -588,11 +549,10 @@
             dma(9), dma(8), dma(1), dma(8), dma(8), dma(8), dma(8), dma(16), dma(16), dma(16), dma(16), dma(6),
         ],
         compiler_params=pltpu.CompilerParams(
-            collective_id=0, has_side_effects=True, vmem_limit_bytes=60 * 1024 * 1024
+            collective_id=0, has_side_effects=True, vmem_limit_bytes=40 * 1024 * 1024
         ),
         name="step",
     )(queries, keys, values, grad_a, grad_b, imports, block_ids)
-    return finish(*outputs)
 
 
 def solution(mesh):

time: 93.4 us -> 100 us (1.071)
  local copies, waits for them, and re-layouts: 0 us -> 9.24 us
  Pallas kernels: 91.8 us -> 89.2 us
    unnamed x0 -> x17, local copies, waits for them, and re-layouts: none -> 9.24 us
    pallas_call x1 -> x0, Pallas kernels: 2.51 us -> none  [finish(): pl.pallas_call(finish_kernel, out_shape=tuple((jax.ShapeDtypeStruct(a.sha...]
where the time goes in v6:
time: 100 us; the launch traced here: 99.1 us
  Pallas kernels  89.2 us (89%)
  local copies, waits for them, and re-layouts  9.24 us (9%)
    pallas_call x1, Pallas kernels, on_device(): pl.pallas_call(step_kernel, out_shape=(jax.ShapeDtypeStruct(grad_a.shape,...  89.2 us
    unnamed x17, local copies, waits for them, and re-layouts  9.24 us

profile of v6, /device:TPU:36, one launch (start us, length us, event | category | flops | bytes accessed | tf_op | source)
XLA Modules:
  0.0 99.1 jit_solution(13575790908986774406)
XLA Ops:
  0.6 0.0 copy-start
  0.6 1.3 %copy-done = bf16[2,1,128,2560]{3,2,1,0:T(8,128)(2,1)S(1)} copy-done((bf16[2,1,128,2560]{3,2,1,0:T(8,128)(2,1)S(1)}, bf16[2,1,128,2560]{3,2,1,0:T(8,128)(2,1)}, u32[]{:S(2)}) %copy-start) | copy-done | bytes 1310744
  1.9 0.0 copy-start.1
  2.0 1.1 %copy-done.1 = bf16[1,128,2560]{2,1,0:T(8,128)(2,1)S(1)} copy-done((bf16[1,128,2560]{2,1,0:T(8,128)(2,1)S(1)}, bf16[1,128,2560]{2,1,0:T(8,128)(2,1)}, u32[]{:S(2)}) %copy-start.1) | copy-done | bytes 655384
  3.0 0.0 copy-start.2
  3.0 1.1 %copy-done.2 = bf16[1,128,2560]{2,1,0:T(8,128)(2,1)S(1)} copy-done((bf16[1,128,2560]{2,1,0:T(8,128)(2,1)S(1)}, bf16[1,128,2560]{2,1,0:T(8,128)(2,1)}, u32[]{:S(2)}) %copy-start.2) | copy-done | bytes 655384
  4.1 0.0 copy-start.3
  4.1 0.9 copy-done.3
  5.1 0.0 copy-start.4
  5.1 0.9 copy-done.4
  6.0 0.0 copy-start.5
  6.0 0.7 copy-done.5
  6.7 0.0 copy-start.6
  6.7 0.7 copy-done.6
  7.4 89.2 %step.1 = (bf16[1,128,2560]{2,1,0:T(8,128)(2,1)S(1)}, bf16[1,128,2560]{2,1,0:T(8,128)(2,1)S(1)}, bf16[2,1,128,1024]{3,2,1,0:T(8,128)(2,1)S(1)}) custom-call(bf16[2,1,128,2560]{3,2,1,0:T(8,128)(2,1)S(1)} %copy-done, bf16[2,1,128,512]{3,2,1,0:T(8,128)(2,1)S(1)} %copy-done.3, bf16[2,1,128,512]{3,2,1,0:T(8,128)(2,1)S(1)} %copy-done.4, ...), custom_call_target="tpu_custom_call" | custom-call | tf_op jit(solution)/shard_map/step/pallas_call | solution.py:531
  96.7 0.8 copy.13
  97.5 0.8 copy.14
  98.4 0.8 copy.15
Async XLA Ops:
  0.6 1.3 %copy-start = (bf16[2,1,128,2560]{3,2,1,0:T(8,128)(2,1)S(1)}, bf16[2,1,128,2560]{3,2,1,0:T(8,128)(2,1)}, u32[]{:S(2)}) copy-start(bf16[2,1,128,2560]{3,2,1,0:T(8,128)(2,1)} %queries.1) | copy-start | bytes 3932164
  1.9 1.1 %copy-start.1 = (bf16[1,128,2560]{2,1,0:T(8,128)(2,1)S(1)}, bf16[1,128,2560]{2,1,0:T(8,128)(2,1)}, u32[]{:S(2)}) copy-start(bf16[1,128,2560]{2,1,0:T(8,128)(2,1)} %grad_a.1) | copy-start | bytes 1966084
  3.0 1.1 %copy-start.2 = (bf16[1,128,2560]{2,1,0:T(8,128)(2,1)S(1)}, bf16[1,128,2560]{2,1,0:T(8,128)(2,1)}, u32[]{:S(2)}) copy-start(bf16[1,128,2560]{2,1,0:T(8,128)(2,1)} %grad_b.1) | copy-start | bytes 1966084
  4.1 0.9 copy-start.3
  5.1 0.9 copy-start.4
  6.0 0.7 copy-start.5
  6.7 0.7 copy-start.6

commit v7 on v5

--- a/solution.py
+++ b/solution.py
@@ -19,7 +19,6 @@
 LISTED = 8
 CHUNKS = LISTED // 2
 FORWARD_AT = 2
-PIECES = 4
 RELAY_AT = 1
 SCALE = 1.0 / math.sqrt(HEAD)
 EXP2_SCALE = SCALE * math.log2(math.e)
@@ -170,6 +169,13 @@
         where = ((m * 2 + to_up) * 3 + index) * NY + piece
         return remote(ref, ref, z_send.at[where], z_recv.at[where], up if to_up else down)
 
+    def z_first(to_up, part):
+        where = (to_up * 3 + part) * NY + y
+        return remote(
+            (keys, values)[part].at[0, 0, :, cols(y, HEAD)], kv_a.at[z, part, y],
+            z_send.at[where], z_recv.at[where], up if to_up else down,
+        )
+
     def spread_piece(m, piece):
         for to_up, part in ((1, 0), (0, 1), (1, 1), (0, 0)):
             z_copy(m, to_up, part, part, z, piece).start()
@@ -220,10 +226,9 @@
             )
             wide_copies[w, d].start()
 
+    for to_up, part in ((1, 0), (0, 1), (1, 1), (0, 0)):
+        z_first(to_up, part).start()
     start_kv(0)
-    for part in range(2):
-        kv_own[0, part].wait()
-    spread_piece(0, y)
     start_kv(1)
     start_wide(0)
     start_wide(1)
@@ -244,6 +249,9 @@
                 z_copy(m, to_up, 2, part, owner, piece).start()
 
     def wait_spread(m):
+        if m == 0:
+            for part in range(2):
+                kv_own[0, part].wait()
         for b in range(NY):
             z_copy(m, 1, 1, 1, z, b).wait_recv()
             z_copy(m, 0, 0, 0, z, b).wait_recv()
@@ -522,20 +530,14 @@
 
 def finish_kernel(*refs):
     sources, targets, held, sem_in, sem_out = refs[:3], refs[3:6], refs[6:9], refs[9], refs[10]
-    incoming, outgoing = [], []
-    for k, (source, target, buffer) in enumerate(zip(sources, targets, held)):
-        rows = ROWS // PIECES
-        for lead in range(source.shape[0]):
-            for p in range(PIECES):
-                middle = (0,) * (len(source.shape) - 3)
-                at = (lead,) + middle + (pl.ds(p * rows, rows),)
-                n = len(incoming)
-                incoming.append(
-                    pltpu.make_async_copy(source.at[at], buffer.at[at], sem_in.at[n])
-                )
-                outgoing.append(
-                    pltpu.make_async_copy(buffer.at[at], target.at[at], sem_out.at[n])
-                )
+    incoming = [
+        pltpu.make_async_copy(source, buffer, sem_in.at[k])
+        for k, (source, buffer) in enumerate(zip(sources, held))
+    ]
+    outgoing = [
+        pltpu.make_async_copy(buffer, target, sem_out.at[k])
+        for k, (buffer, target) in enumerate(zip(held, targets))
+    ]
     for copy in incoming:
         copy.start()
     for copy, later in zip(incoming, outgoing):
@@ -553,7 +555,7 @@
         in_specs=[whole] * 3,
         out_specs=(whole,) * 3,
         scratch_shapes=[pltpu.VMEM(a.shape, a.dtype) for a in arrays]
-        + [pltpu.SemaphoreType.DMA((4 * PIECES,)), pltpu.SemaphoreType.DMA((4 * PIECES,))],
+        + [pltpu.SemaphoreType.DMA((3,)), pltpu.SemaphoreType.DMA((3,))],
         name="finish",
     )(*arrays)
 

time: 93.4 us -> 93.4 us (level)
  no operation moved by 1% of the time
where the time goes in v7:
time: 93.4 us; the launch traced here: 93.2 us
  Pallas kernels  92.5 us (99%)
    pallas_call x1, Pallas kernels, on_device(): pl.pallas_call(step_kernel, out_shape=(jax.ShapeDtypeStruct(grad_a.shape,...  90.2 us
    pallas_call x1, Pallas kernels, finish(): pl.pallas_call(finish_kernel, out_shape=tuple((jax.ShapeDtypeStruct(a.sha...  2.36 us

profile of v7, /device:TPU:36, one launch (start us, length us, event | category | flops | bytes accessed | tf_op | source)
XLA Modules:
  0.0 93.2 jit_solution(7395981705800544333)
XLA Ops:
  0.6 90.2 %step.1 = (bf16[1,128,2560]{2,1,0:T(8,128)(2,1)}, bf16[1,128,2560]{2,1,0:T(8,128)(2,1)}, bf16[2,1,128,1024]{3,2,1,0:T(8,128)(2,1)}) custom-call(bf16[2,1,128,2560]{3,2,1,0:T(8,128)(2,1)} %queries.1, bf16[2,1,128,512]{3,2,1,0:T(8,128)(2,1)} %keys.1, bf16[2,1,128,512]{3,2,1,0:T(8,128)(2,1)} %values.1, bf16[1,128,2560]{2,1,0:T(8,128)(2,1)} %grad_a.1, ...), custom_call_target="tpu_custom_call" | custom-call | tf_op jit(solution)/shard_map/step/pallas_call | solution.py:572
  90.8 2.4 %finish.1 = (bf16[1,128,2560]{2,1,0:T(8,128)(2,1)}, bf16[1,128,2560]{2,1,0:T(8,128)(2,1)}, bf16[2,1,128,1024]{3,2,1,0:T(8,128)(2,1)}) custom-call(bf16[1,128,2560]{2,1,0:T(8,128)(2,1)} %get-tuple-element.6.refs_0_, bf16[1,128,2560]{2,1,0:T(8,128)(2,1)} %get-tuple-element.7.refs_1_, bf16[2,1,128,1024]{3,2,1,0:T(8,128)(2,1)} %get-tuple-element.8.refs_2_), custom_call_target="tpu_custom_call" | custom-call | tf_op jit(solution)/shard_map/finish/pallas_call | solution.py:552

commit v8 on v7

--- a/solution.py
+++ b/solution.py
@@ -19,7 +19,7 @@
 LISTED = 8
 CHUNKS = LISTED // 2
 FORWARD_AT = 2
-RELAY_AT = 1
+RELAY_AT = 2
 SCALE = 1.0 / math.sqrt(HEAD)
 EXP2_SCALE = SCALE * math.log2(math.e)
 NEG = -1e30

time: 93.4 us -> 94.5 us (1.012); the launches traced: 93.2 us -> 93.2 us
  no operation moved by 1% of the time
where the time goes in v8:
time: 94.5 us; the launch traced here: 93.2 us
  Pallas kernels  92.5 us (98%)
    pallas_call x1, Pallas kernels, on_device(): pl.pallas_call(step_kernel, out_shape=(jax.ShapeDtypeStruct(grad_a.shape,...  90.2 us
    pallas_call x1, Pallas kernels, finish(): pl.pallas_call(finish_kernel, out_shape=tuple((jax.ShapeDtypeStruct(a.sha...  2.36 us

profile of v8, /device:TPU:36, one launch (start us, length us, event | category | flops | bytes accessed | tf_op | source)
XLA Modules:
  0.0 93.2 jit_solution(10306512372637782460)
XLA Ops:
  0.6 90.2 %step.1 = (bf16[1,128,2560]{2,1,0:T(8,128)(2,1)}, bf16[1,128,2560]{2,1,0:T(8,128)(2,1)}, bf16[2,1,128,1024]{3,2,1,0:T(8,128)(2,1)}) custom-call(bf16[2,1,128,2560]{3,2,1,0:T(8,128)(2,1)} %queries.1, bf16[2,1,128,512]{3,2,1,0:T(8,128)(2,1)} %keys.1, bf16[2,1,128,512]{3,2,1,0:T(8,128)(2,1)} %values.1, bf16[1,128,2560]{2,1,0:T(8,128)(2,1)} %grad_a.1, ...), custom_call_target="tpu_custom_call" | custom-call | tf_op jit(solution)/shard_map/step/pallas_call | solution.py:572
  90.8 2.4 %finish.1 = (bf16[1,128,2560]{2,1,0:T(8,128)(2,1)}, bf16[1,128,2560]{2,1,0:T(8,128)(2,1)}, bf16[2,1,128,1024]{3,2,1,0:T(8,128)(2,1)}) custom-call(bf16[1,128,2560]{2,1,0:T(8,128)(2,1)} %get-tuple-element.6.refs_0_, bf16[1,128,2560]{2,1,0:T(8,128)(2,1)} %get-tuple-element.7.refs_1_, bf16[2,1,128,1024]{3,2,1,0:T(8,128)(2,1)} %get-tuple-element.8.refs_2_), custom_call_target="tpu_custom_call" | custom-call | tf_op jit(solution)/shard_map/finish/pallas_call | solution.py:552

commit v9 on v7

--- a/solution.py
+++ b/solution.py
@@ -351,14 +351,13 @@
         def _():
             dq_copy(m, y, i).start()
 
-    def combine(m, dkv):
+    def combine(m, dkv, part):
         def one(slot, nothing):
             places = [where_part[(m * NY + i) * BLOCKS + slot] for i in range(NY)]
-            for part in range(2):
-                value = parts[places[0], part]
-                for at in places[1:]:
-                    value = value + parts[at, part]
-                dkv[lax.rem(slot, NZ), part, slot // NZ] = value.astype(BF16)
+            value = parts[places[0], part]
+            for at in places[1:]:
+                value = value + parts[at, part]
+            dkv[lax.rem(slot, NZ), part, slot // NZ] = value.astype(BF16)
             return nothing
 
         lax.fori_loop(0, BLOCKS, one, 0)
@@ -385,8 +384,12 @@
         )
 
     def reduce_start(m):
-        for index in range(4):
-            r_copy(m, index).start()
+        combine(m, dkvs[m], 1)
+        r_copy(m, 1).start()
+        r_copy(m, 2).start()
+        combine(m, dkvs[m], 0)
+        r_copy(m, 0).start()
+        r_copy(m, 3).start()
 
     def reduce_relay(m):
         relay, total, dkv = relays[m], totals[m], dkvs[m]
@@ -469,7 +472,6 @@
         return nothing
 
     lax.fori_loop(0, NY, turn_a, 0)
-    combine(0, dkv_a)
     pass_on(NY)
     reduce_start(0)
     wait_spread(1)
@@ -496,7 +498,6 @@
         return nothing
 
     lax.fori_loop(0, NY, turn_b, 0)
-    combine(1, dkv_b)
     reduce_start(1)
     reduce_end(0)
     reduce_relay(1)

time: 93.4 us -> 96.2 us (1.030)
  the two profiles are of different devices: /device:TPU:36 before, /device:TPU:16 now
where the time goes in v9:
time: 96.2 us; the launch traced here: 96 us
  Pallas kernels  95.4 us (99%)
    pallas_call x1, Pallas kernels, on_device(): pl.pallas_call(step_kernel, out_shape=(jax.ShapeDtypeStruct(grad_a.shape,...  93 us
    pallas_call x1, Pallas kernels, finish(): pl.pallas_call(finish_kernel, out_shape=tuple((jax.ShapeDtypeStruct(a.sha...  2.36 us

profile of v9, /device:TPU:16, one launch (start us, length us, event | category | flops | bytes accessed | tf_op | source)
XLA Modules:
  0.0 96.0 jit_solution(9225717293028057883)
XLA Ops:
  0.6 93.0 %step.1 = (bf16[1,128,2560]{2,1,0:T(8,128)(2,1)}, bf16[1,128,2560]{2,1,0:T(8,128)(2,1)}, bf16[2,1,128,1024]{3,2,1,0:T(8,128)(2,1)}) custom-call(bf16[2,1,128,2560]{3,2,1,0:T(8,128)(2,1)} %queries.1, bf16[2,1,128,512]{3,2,1,0:T(8,128)(2,1)} %keys.1, bf16[2,1,128,512]{3,2,1,0:T(8,128)(2,1)} %values.1, bf16[1,128,2560]{2,1,0:T(8,128)(2,1)} %grad_a.1, ...), custom_call_target="tpu_custom_call" | custom-call | tf_op jit(solution)/shard_map/step/pallas_call | solution.py:573
  93.7 2.4 %finish.1 = (bf16[1,128,2560]{2,1,0:T(8,128)(2,1)}, bf16[1,128,2560]{2,1,0:T(8,128)(2,1)}, bf16[2,1,128,1024]{3,2,1,0:T(8,128)(2,1)}) custom-call(bf16[1,128,2560]{2,1,0:T(8,128)(2,1)} %get-tuple-element.6.refs_0_, bf16[1,128,2560]{2,1,0:T(8,128)(2,1)} %get-tuple-element.7.refs_1_, bf16[2,1,128,1024]{3,2,1,0:T(8,128)(2,1)} %get-tuple-element.8.refs_2_), custom_call_target="tpu_custom_call" | custom-call | tf_op jit(solution)/shard_map/finish/pallas_call | solution.py:553
